TPU v7x, 512 devices: a whole 4x4x16 slice. The times are simulated.
512 devices in a mesh: chan: 64 (over y, z_lo, core), lag: 4 (over x), seg: 2 (over z_hi).
Axes of the slice: x: 4, y: 4, z: 16 (z_hi: 2, z_lo: 8; z = z_hi * 8 + z_lo), core: 2. Of those that a mesh axis runs over, the one named last changes fastest.
Arguments:
- records_owned: float32 [8192, 2, 1024], P('chan', 'seg', 'lag'), may hold values from -6 to 6
- section_list: int32 [8192], replicated, may hold values from 0 to 8191, as said below
- ref_index: int32 [64], replicated, may hold values from 0 to 8191, as said below
Outputs:
- correlations: float32 [8192, 8192], P(('chan', 'seg'), 'lag')
Inputs may be any that keep to these rules, and one draw needn't show every extreme that they name: `section_list`: each value names a channel once. The 128 rows of each owner name exactly 2 channels of every channel block (channels b*128 to (b+1)*128 - 1). `ref_index`: distinct channel numbers.
All inputs are finite; a program needn't handle non-finite values.
Results may differ from a plain program's by a relative error of at most 0.000098.
Values sent between devices are 32-bit elements; how exact they have to be, the bound alone decides.
A program may use at most 64 MiB of HBM per device.

v0:
```python
import math

import jax
import jax.numpy as jnp
from jax import lax
from jax.sharding import PartitionSpec as P

LAGS = 128
SAMPLES = 2048


def from_behind(value, axis, steps):
    count = lax.axis_size(axis)
    first, last = (max(0, -steps), min(count, count - steps))
    return lax.ppermute(value, axis, [(source, source + steps) for source in range(first, last)])


def shifted_panel(panel_rows, lag_width):
    columns = panel_rows.T
    stacked = [
        jnp.pad(columns, ((offset, lag_width - offset), (0, 0))) for offset in range(lag_width)
    ]
    return jnp.stack(stacked, axis=1).reshape(
        columns.shape[0] + lag_width, lag_width * columns.shape[1]
    )


def shards(records_owned, section_list, ref_index):
    block_count = lax.axis_size("chan")
    own_block = lax.axis_index("chan")
    block_rows = records_owned.shape[0]
    peer_rows = block_rows // block_count
    owner_lists = section_list.reshape(block_count, block_rows)
    own_list = lax.dynamic_slice_in_dim(owner_lists, own_block, 1, 0)[0]
    send_order = jnp.argsort(own_list // block_rows, stable=True)
    pieces = records_owned[:, 0, :]
    elsewhere = (owner_lists // block_rows != own_block).astype(jnp.int32)
    picked = jnp.argsort(elsewhere, axis=1, stable=True)[:, :peer_rows]
    arrived_ids = (
        jnp.take_along_axis(owner_lists, picked, axis=1).reshape(block_rows)
        - own_block * block_rows
    )
    placing = jnp.argsort(arrived_ids)
    joined = lax.all_gather(pieces, "lag", axis=1, tiled=True)
    sorted_rows = joined[send_order].reshape(block_count, peer_rows, joined.shape[1])
    arrived = lax.all_to_all(sorted_rows, "chan", split_axis=0, concat_axis=0, tiled=True)
    placed = arrived.reshape(block_rows, arrived.shape[2])[placing]
    lag_width = LAGS // lax.axis_size("lag")
    lag_start = lax.axis_index("lag") * lag_width
    segment_index = lax.axis_index("seg")
    terms = SAMPLES - LAGS
    segment_length = placed.shape[1]
    channel_ids = own_block * block_rows + jnp.arange(block_rows, dtype=jnp.int32)
    selector = (ref_index[:, None] == channel_ids[None, :]).astype(jnp.float32)
    panel_part = jnp.dot(
        selector, placed, precision=lax.Precision.HIGHEST, preferred_element_type=jnp.float32
    )
    panel = lax.psum(panel_part, "chan")
    sample_times = segment_index * segment_length + jnp.arange(segment_length, dtype=jnp.int32)
    panel = jnp.where((sample_times < terms)[None, :], panel, 0.0)
    following = from_behind(placed[:, :LAGS], "seg", -1)
    extended = jnp.concatenate([placed, following], axis=1)
    window = lax.dynamic_slice_in_dim(extended, lag_start, segment_length + lag_width, 1)
    toeplitz = shifted_panel(panel, lag_width)
    summed = lax.psum_scatter(
        jnp.dot(
            window, toeplitz, precision=lax.Precision.HIGHEST, preferred_element_type=jnp.float32
        ),
        "seg",
        scatter_dimension=0,
        tiled=True,
    )
    return summed / math.sqrt(terms)


def solution(mesh):
    return jax.shard_map(
        shards,
        mesh=mesh,
        in_specs=(P("chan", "seg", "lag"), P(), P()),
        out_specs=P(("chan", "seg"), "lag"),
        check_vma=False,
    )
```

profile of v0, /device:TPU:1, one launch (start us, length us, event | category | flops | bytes accessed | tf_op | source)
XLA Modules:
  0.0 950.7 jit_solution(17247490633266252985)
XLA Ops:
  6.5 0.8 and_select_fusion
  7.3 2.5 sort.51
  9.9 0.9 copy.7
  10.8 11.1 %all-gather = f32[128,1,1024]{2,0,1:T(8,128)S(1)} all-gather(f32[128,1,256]{2,0,1:T(8,128)S(1)} %copy.7), channel_id=2, replica_groups=mesh['chan'=64,'lag'=4,'seg'=2] {'lag'}, dimensions={2}, use_global_device_ids=true | all-gather | bytes 655360 | tf_op jit(solution)/shard_map/all_gather | solution.py:44
  21.9 0.8 gather_fusion
  22.7 1.1 reshape.39
  23.8 19.3 %all-to-all-start = ((f32[64,2,1024]{2,1,0:T(2,128)}), f32[64,2,1024]{2,1,0:T(2,128)S(1)}, u32[]{:S(2)}, u32[]{:S(2)}) async-start(f32[64,2,1024]{2,1,0:T(2,128)} %reshape.39), calls=%async_computation | async-start | bytes 1048576 | tf_op jit(solution)/shard_map/all_to_all | solution.py:46
  43.1 1.4 fusion.7
  44.5 0.6 iota.26
  45.2 4.3 sort.55.cloned.1.call-done
  49.5 0.8 clamp_shift-left_fusion
  50.4 0.1 reshape.59
  50.6 1.2 gather_fusion.2
  52.2 2.6 sort.53
  54.8 17.8 %all-to-all-done = f32[64,2,1024]{2,1,0:T(2,128)S(1)} async-done(((f32[64,2,1024]{2,1,0:T(2,128)}), f32[64,2,1024]{2,1,0:T(2,128)S(1)}, u32[]{:S(2)}, u32[]{:S(2)}) %all-to-all-start) | async-done | bytes 524320 | tf_op jit(solution)/shard_map/all_to_all | solution.py:46
  72.7 0.4 reshape.40
  73.0 0.8 gather_fusion.1
  73.8 1.0 fusion.8
  75.0 1.5 collective-permute-start
  76.5 775.5 %all-reduce.34.cloned.1.call-done = f32[64,1024]{1,0:T(8,128)} async-done(((f32[64,1024]{1,0:T(8,128)}), f32[64,1024]{1,0:T(8,128)}) %all-reduce.34.cloned.1.call-update) | async-done | bytes 262160 | tf_op jit(solution)/shard_map/psum | solution.py:58
  852.0 1.0 select_bitcast_fusion
  853.1 0.1 bitcast_dynamic-update-slice_fusion.29
  853.3 0.1 bitcast_dynamic-update-slice_fusion.28
  853.4 0.1 bitcast_dynamic-update-slice_fusion.27
  853.5 0.1 bitcast_dynamic-update-slice_fusion.26
  853.7 0.1 bitcast_dynamic-update-slice_fusion.25
  853.8 0.1 bitcast_dynamic-update-slice_fusion.24
  854.0 0.1 bitcast_dynamic-update-slice_fusion.23
  854.1 0.1 bitcast_dynamic-update-slice_fusion.22
  854.3 0.1 bitcast_dynamic-update-slice_fusion.21
  854.4 0.1 bitcast_dynamic-update-slice_fusion.20
  854.7 0.1 bitcast_dynamic-update-slice_fusion.18
  855.0 0.1 bitcast_dynamic-update-slice_fusion.16
  855.2 0.1 bitcast_dynamic-update-slice_fusion.15
  855.3 0.1 bitcast_dynamic-update-slice_fusion.14
  855.4 0.1 bitcast_dynamic-update-slice_fusion.13
  855.6 0.1 bitcast_dynamic-update-slice_fusion.12
  855.7 0.1 bitcast_dynamic-update-slice_fusion.11
  855.9 0.1 bitcast_dynamic-update-slice_fusion.10
  856.0 0.1 bitcast_dynamic-update-slice_fusion.9
  856.2 0.1 bitcast_dynamic-update-slice_fusion.8
  856.3 0.1 bitcast_dynamic-update-slice_fusion.7
  856.6 0.1 bitcast_dynamic-update-slice_fusion.5
  856.9 0.1 bitcast_dynamic-update-slice_fusion.3
  857.2 0.1 bitcast_dynamic-update-slice_fusion.1
  857.5 10.7 %fusion = f32[128,2048]{1,0:T(8,128)} fusion(f32[1056,2048]{0,1:T(8,128)S(1)} %bitcast.83, s32[]{:T(128)S(6)} %select_n.43, f32[128,128]{1,0:T(8,128)S(1)} %collective-permute-done, f32[128,1024]{1,0:T(8,128)S(1)} %gather_fusion.1), kind=kOutput, calls=%fused_computation.4 | convolution fusion | flops 3322023936 | bytes 10289156 | tf_op jit(solution)/shard_map/dot_general | solution.py:66
  868.2 74.1 %reduce-scatter.2.cloned.1.call-done = f32[64,2048]{1,0:T(8,128)} async-done(((f32[128,2048]{1,0:T(8,128)}), f32[64,2048]{1,0:T(8,128)}) %reduce-scatter.2.cloned.1.call-update) | async-done | bytes 524304 | tf_op jit(solution)/shard_map/reduce_scatter | solution.py:65
  942.3 1.9 broadcast_multiply_fusion
  (36 shorter events, 1.7 us)
Async XLA Ops:
  6.5 44.0 %copy-start = (s32[8192]{0:T(1024)S(1)}, s32[8192]{0:T(1024)}, u32[]{:S(2)}) copy-start(s32[8192]{0:T(1024)} %param.4) | copy-start | bytes 98308
  23.8 48.9 %all-to-all-start = ((f32[64,2,1024]{2,1,0:T(2,128)}), f32[64,2,1024]{2,1,0:T(2,128)S(1)}, u32[]{:S(2)}, u32[]{:S(2)}) async-start(f32[64,2,1024]{2,1,0:T(2,128)} %reshape.39), calls=%async_computation | async-start | bytes 1048576 | tf_op jit(solution)/shard_map/all_to_all | solution.py:46
  43.0 6.4 sort.55.cloned.1.call-start
  45.1 806.9 %all-reduce.34.cloned.1.call-start = ((), (), s32[]{:S(2)}) async-start(), calls=%async_computation.2 | async-start | bytes 524288 | tf_op jit(solution)/shard_map/psum | solution.py:58
  50.6 1.4 copy-start.1
  50.6 23.2 %copy-start.2 = (s32[64]{0:T(128)S(1)}, s32[64]{0:T(128)}, u32[]{:S(2)}) copy-start(s32[64]{0:T(128)} %param.5) | copy-start | bytes 772
  74.9 867.4 %reduce-scatter.2.cloned.1.call-start = ((), (), s32[]{:S(2)}) async-start(), calls=%async_computation.3 | async-start | bytes 1572864 | tf_op jit(solution)/shard_map/reduce_scatter | solution.py:65
  75.0 782.5 %collective-permute-start = (f32[128,128]{1,0:T(8,128)S(1)}, f32[128,128]{1,0:T(8,128)S(1)}, u32[]{:S(2)}, u32[]{:S(2)}) collective-permute-start(f32[128,128]{1,0:T(8,128)S(1)} %slice.14), channel_id=1, source_target_pairs={{1,0},{3,2},{5,4},{7,6},{9,8},{11,10},{13,12},{15,14},{17,16},{19,... | collective-permute-start | bytes 196616 | tf_op jit(solution)/shard_map/ppermute | solution.py:15
Sparse Core Ops, SparseCore 0:
  46.1 3.0 sort.57.cloned.1.call-done
  75.0 776.9 all-reduce.33
  868.3 73.9 reduce-scatter.1
  (1 shorter events, 0.0 us)
where the time goes:
time: 951 us
  waiting for transfers between devices  867 us (91%)
  starting transfers between devices  20.8 us (2%)
  local copies, waits for them, and re-layouts  15.1 us (2%)
  between operations  13.5 us (1%)
  matrix products  11.7 us (1%)
  blocking collectives  11.1 us (1%)
  other arithmetic  11 us (1%)
    psum x1, waiting for transfers between devices, shards(): panel = lax.psum(panel_part, 'chan')  775 us
    reduce_scatter x1, waiting for transfers between devices, shards(): lax.psum_scatter(jnp.dot(window, toeplitz, precision=lax.Precision.HIGHES...  74.1 us
    all_to_all x1, starting transfers between devices, shards(): lax.all_to_all(sorted_rows, 'chan', split_axis=0, concat_axis=0, tiled=True)  19.3 us
  transfers between devices with their start and end apart: 4, of which 3 were waited for; matrix products, arithmetic and copies ran while one was open for 1% of the time, Pallas kernels for 0%

commit v1 on v0

v1 whole, which is shorter than its diff:
```python
import math

import jax
import jax.numpy as jnp
from jax import lax
from jax.experimental import pallas as pl
from jax.experimental.pallas import tpu as pltpu
from jax.sharding import PartitionSpec as P

LAGS = 128
SAMPLES = 2048
REF = 64
TERMS = SAMPLES - LAGS
LANES = 128
TILES = SAMPLES // LANES
COLUMN_LAGS = 4


def split(value):
    high = value.astype(jnp.bfloat16)
    return high, (value - high.astype(jnp.float32)).astype(jnp.bfloat16)


def transposed_dot(left, right):
    return lax.dot_general(
        left, right, (((1,), (1,)), ((), ())), preferred_element_type=jnp.float32
    )


def correlate(series_ref, panel_ref, out_ref, windows_high, windows_low, shifts_high, shifts_low):
    lag_width = LAGS // lax.axis_size("lag")
    rows = series_ref.shape[1]
    groups = lag_width // COLUMN_LAGS
    start = lax.axis_index("lag") * lag_width
    panel = jnp.concatenate(
        [panel_ref[tile] for tile in range(TERMS // LANES)]
        + [jnp.zeros((REF, LANES), jnp.float32)] * (TILES - TERMS // LANES),
        axis=1,
    )
    panel = pltpu.roll(panel, start, 1)
    for shift in range(COLUMN_LAGS):
        high, low = split(pltpu.roll(panel, shift, 1) if shift else panel)
        shifts_high[pl.ds(shift * REF, REF), :] = high
        shifts_low[pl.ds(shift * REF, REF), :] = low
    series = jnp.concatenate([series_ref[tile] for tile in range(TILES)], axis=1)
    for group in range(groups):
        lag = group * COLUMN_LAGS
        high, low = split(pltpu.roll(series, SAMPLES - lag, 1) if lag else series)
        windows_high[pl.ds(group * rows, rows), :] = high
        windows_low[pl.ds(group * rows, rows), :] = low
    total = (
        transposed_dot(windows_high[...], shifts_high[...])
        + transposed_dot(windows_high[...], shifts_low[...])
        + transposed_dot(windows_low[...], shifts_high[...])
    )
    width = COLUMN_LAGS * REF
    for group in range(groups):
        out_ref[:, pl.ds(group * width, width)] = total[group * rows : (group + 1) * rows] * (
            1.0 / math.sqrt(TERMS)
        )


def select_rows(one_hot, values):
    return jnp.dot(
        one_hot.astype(jnp.float32),
        values,
        precision=lax.Precision.HIGHEST,
        preferred_element_type=jnp.float32,
    )


def shards(records_owned, section_list, ref_index):
    blocks = lax.axis_size("chan")
    own_block = lax.axis_index("chan")
    segment = lax.axis_index("seg")
    block_rows = records_owned.shape[0]
    half_rows = block_rows // lax.axis_size("seg")
    samples = records_owned.shape[2]
    owner_lists = section_list.reshape(blocks, block_rows)
    own_list = lax.dynamic_slice_in_dim(owner_lists, own_block, 1, 0)[0]
    list_block = own_list // block_rows
    behind = (list_block[:, None] == list_block[None, :]) & (own_list[:, None] < own_list[None, :])
    rank = jnp.sum(behind.astype(jnp.int32), axis=0)
    wanted = jnp.arange(blocks)
    chosen = jnp.stack(
        [
            (wanted[:, None] == list_block[None, :]) & (rank[None, :] == 0),
            (wanted[:, None] == list_block[None, :]) & (rank[None, :] == 1),
            ref_index[:, None] == own_list[None, :],
        ],
        axis=1,
    ).reshape(3 * blocks, block_rows)
    outgoing = select_rows(chosen, records_owned[:, 0, :]).reshape(blocks, 3, samples)
    arrived = lax.all_to_all(outgoing, "chan", split_axis=0, concat_axis=0, tiled=True)
    inside = owner_lists // block_rows == own_block
    first = jnp.min(jnp.where(inside, owner_lists, blocks * block_rows), axis=1)
    second = jnp.max(jnp.where(inside, owner_lists, -1), axis=1)
    ids = jnp.stack([first, second, jnp.full_like(first, -1)], axis=1).reshape(3 * blocks)
    places = jnp.arange(block_rows)
    turned = own_block * block_rows + (places + segment * half_rows) % block_rows
    place = turned[:, None] == ids[None, :]
    panel_place = (jnp.arange(3 * blocks) % 3 == 2)[None, :]
    placed = select_rows(
        jnp.concatenate([place, panel_place], axis=0), arrived.reshape(3 * blocks, samples)
    )
    mine = placed[:half_rows]
    theirs = placed[half_rows:block_rows]
    swapped = lax.ppermute(theirs, "seg", [(0, 1), (1, 0)])
    pair = jnp.stack([mine, swapped])
    pair = jnp.where(segment == 0, pair, pair[::-1])
    panel_rows = lax.all_gather(placed[block_rows:], ("chan",), axis=0, tiled=True)
    series = lax.all_gather(pair, "lag", axis=1)
    panel = lax.all_gather(panel_rows, ("seg", "lag"), axis=0)
    parts = samples // LANES
    series = series.reshape(TILES // parts, half_rows, parts, LANES)
    series = series.transpose(0, 2, 1, 3).reshape(TILES, half_rows, LANES)
    panel = panel.reshape(TILES // parts, REF, parts, LANES)
    panel = panel.transpose(0, 2, 1, 3).reshape(TILES, REF, LANES)
    lag_width = LAGS // lax.axis_size("lag")
    groups = lag_width // COLUMN_LAGS
    return pl.pallas_call(
        correlate,
        out_shape=jax.ShapeDtypeStruct((half_rows, lag_width * REF), jnp.float32),
        in_specs=[pl.BlockSpec(memory_space=pltpu.VMEM)] * 2,
        out_specs=pl.BlockSpec(memory_space=pltpu.VMEM),
        scratch_shapes=[pltpu.VMEM((groups * half_rows, SAMPLES), jnp.bfloat16)] * 2
        + [pltpu.VMEM((COLUMN_LAGS * REF, SAMPLES), jnp.bfloat16)] * 2,
        compiler_params=pltpu.CompilerParams(vmem_limit_bytes=32 * 1024 * 1024),
        name="correlate",
    )(series, panel)


def solution(mesh):
    return jax.shard_map(
        shards,
        mesh=mesh,
        in_specs=(P("chan", "seg", "lag"), P(), P()),
        out_specs=P(("chan", "seg"), "lag"),
        check_vma=False,
    )
```

time: 951 us -> 253 us (0.27)
  the two profiles are of different devices: /device:TPU:1 before, /device:TPU:2 now
where the time goes in v1:
time: 253 us
  blocking collectives  193 us (76%)
  waiting for transfers between devices  27.6 us (11%)
  starting transfers between devices  22.9 us (9%)
  Pallas kernels  3.65 us (1%)
    all_gather x1, blocking collectives, shards(): lax.all_gather(placed[block_rows:], ('chan',), axis=0, tiled=True)  115 us
    all_gather x1, blocking collectives, shards(): panel = lax.all_gather(panel_rows, ('seg', 'lag'), axis=0)  60.9 us
    all_to_all x1, waiting for transfers between devices, shards(): lax.all_to_all(outgoing, 'chan', split_axis=0, concat_axis=0, tiled=True)  19.4 us
    all_gather x1, blocking collectives, shards(): series = lax.all_gather(pair, 'lag', axis=1)  17.5 us
    all_to_all x1, starting transfers between devices, shards(): lax.all_to_all(outgoing, 'chan', split_axis=0, concat_axis=0, tiled=True)  16.3 us
    ppermute x1, waiting for transfers between devices, shards(): swapped = lax.ppermute(theirs, 'seg', [(0, 1), (1, 0)])  8.25 us
    ppermute x1, starting transfers between devices, shards(): swapped = lax.ppermute(theirs, 'seg', [(0, 1), (1, 0)])  6.58 us
  transfers between devices with their start and end apart: 2, of which 2 were waited for; matrix products, arithmetic and copies ran while one was open for 0% of the time, Pallas kernels for 0%

profile of v1, /device:TPU:2, one launch (start us, length us, event | category | flops | bytes accessed | tf_op | source)
XLA Modules:
  0.0 253.1 jit_solution(15982614766172658776)
XLA Ops:
  0.0 0.7 and_select_fusion.1
  0.7 0.7 fusion.20
  1.4 0.1 convert_reduce_fusion
  1.5 0.0 copy-start.1
  1.5 0.6 copy-done.1
  2.2 0.1 fusion.15
  2.3 1.1 fusion.4
  3.4 0.8 copy.12
  4.2 0.0 copy-start
  4.3 16.3 %all-to-all-start = ((f32[64,3,256]{2,1,0:T(4,128)}), f32[64,3,256]{2,1,0:T(4,128)S(1)}, u32[]{:S(2)}, u32[]{:S(2)}) async-start(f32[64,3,256]{2,1,0:T(4,128)} %copy.12), calls=%async_computation | async-start | bytes 524288 | tf_op jit(solution)/shard_map/all_to_all | solution.py:94
  20.6 0.1 pad.11.clone
  20.6 0.0 copy-done
  20.6 0.1 select_reduce_fusion.1
  20.8 0.1 add_add_fusion
  20.8 0.1 copy.11
  20.9 0.1 eq.127
  21.1 0.1 broadcast_compare_fusion
  21.2 19.4 %all-to-all-done = f32[64,3,256]{2,1,0:T(4,128)S(1)} async-done(((f32[64,3,256]{2,1,0:T(4,128)}), f32[64,3,256]{2,1,0:T(4,128)S(1)}, u32[]{:S(2)}, u32[]{:S(2)}) %all-to-all-start) | async-done | bytes 196640 | tf_op jit(solution)/shard_map/all_to_all | solution.py:94
  40.6 0.1 reshape.247
  40.7 0.2 fusion
  41.0 114.8 %all-gather.2 = f32[64,1,256]{2,1,0:T(1,128)S(1)} all-gather(f32[1,1,256]{2,1,0:T(1,128)S(1)} %slice_bitcast_fusion.1), channel_id=1, replica_groups=mesh['chan'=64,'lag'=4,'seg'=2] {'chan'}, dimensions={0}, use_global_device_ids=true | all-gather | bytes 66560 | tf_op jit(solution)/shard_map/all_gather | solution.py:111
  155.8 60.9 %all-gather.1 = f32[512,256]{1,0:T(8,128)S(1)} all-gather(f32[64,256]{1,0:T(8,128)S(1)} %bitcast.36), channel_id=3, replica_groups=mesh['chan'=64,'lag'=4,'seg'=2] {'seg','lag'}, dimensions={0}, use_global_device_ids=true | all-gather | bytes 589824 | tf_op jit(solution)/shard_map/all_gather | solution.py:113
  216.7 6.6 %collective-permute-start = (f32[64,256]{1,0:T(8,128)S(1)}, f32[64,256]{1,0:T(8,128)S(1)}, u32[]{:S(2)}, u32[]{:S(2)}) collective-permute-start(f32[64,256]{1,0:T(8,128)S(1)} %get-tuple-element.12), channel_id=1, source_target_pairs={{0,1},{1,0},{2,3},{3,2},{4,5},{5,4},{6,7},{7,6},{8,9},{9,8},{10,11... | collective-permute-start | bytes 196616 | tf_op jit(solution)/shard_map/ppermute | solution.py:108
  223.4 8.2 %collective-permute-done = f32[64,256]{1,0:T(8,128)S(1)} collective-permute-done((f32[64,256]{1,0:T(8,128)S(1)}, f32[64,256]{1,0:T(8,128)S(1)}, u32[]{:S(2)}, u32[]{:S(2)}) %collective-permute-start) | collective-permute-done | bytes 65568 | tf_op jit(solution)/shard_map/ppermute | solution.py:108
  231.7 17.5 %all-gather = f32[2,256,256]{2,1,0:T(8,128)S(1)} all-gather(f32[2,64,256]{2,1,0:T(8,128)S(1)} %reverse_select_fusion), channel_id=2, replica_groups=mesh['chan'=64,'lag'=4,'seg'=2] {'lag'}, dimensions={1}, use_global_device_ids=true | all-gather | bytes 655360 | tf_op jit(solution)/shard_map/all_gather | solution.py:112
  249.2 0.3 reshape.248
  249.4 0.1 copy.13
  249.5 3.7 %correlate.1 = f32[64,2048]{1,0:T(8,128)} custom-call(f32[16,64,128]{2,1,0:T(8,128)S(1)} %bitcast.34, f32[16,64,128]{2,1,0:T(8,128)S(1)} %bitcast.33), custom_call_target="tpu_custom_call" | custom-call | tf_op jit(solution)/shard_map/correlate/pallas_call | solution.py:121
  (10 shorter events, 0.2 us)
Async XLA Ops:
  1.5 0.7 copy-start.1
  4.2 16.4 %copy-start = (s32[8192]{0:T(1024)S(1)}, s32[8192]{0:T(1024)}, u32[]{:S(2)}) copy-start(s32[8192]{0:T(1024)} %param.4) | copy-start | bytes 98308
  4.3 36.4 %all-to-all-start = ((f32[64,3,256]{2,1,0:T(4,128)}), f32[64,3,256]{2,1,0:T(4,128)S(1)}, u32[]{:S(2)}, u32[]{:S(2)}) async-start(f32[64,3,256]{2,1,0:T(4,128)} %copy.12), calls=%async_computation | async-start | bytes 524288 | tf_op jit(solution)/shard_map/all_to_all | solution.py:94
  216.7 14.9 %collective-permute-start = (f32[64,256]{1,0:T(8,128)S(1)}, f32[64,256]{1,0:T(8,128)S(1)}, u32[]{:S(2)}, u32[]{:S(2)}) collective-permute-start(f32[64,256]{1,0:T(8,128)S(1)} %get-tuple-element.12), channel_id=1, source_target_pairs={{0,1},{1,0},{2,3},{3,2},{4,5},{5,4},{6,7},{7,6},{8,9},{9,8},{10,11... | collective-permute-start | bytes 196616 | tf_op jit(solution)/shard_map/ppermute | solution.py:108

commit v2 on v1

v2 whole, which is shorter than its diff:
```python
import math

import jax
import jax.numpy as jnp
from jax import lax
from jax.experimental import pallas as pl
from jax.experimental.pallas import tpu as pltpu
from jax.sharding import PartitionSpec as P

MESH = pl.DeviceIdType.MESH
LAGS = 128
SAMPLES = 2048
REF = 64
TERMS = SAMPLES - LAGS
LANES = 128
TILES = SAMPLES // LANES
COLUMN_LAGS = 4
OWNERS = 64
ROWS = 128
HALF = 64
SEGMENTS = 2
LAG_PARTS = 4
Y, Z, CORES = 4, 8, 2
PARTS = 2
SENT = 6


def split(value):
    high = value.astype(jnp.bfloat16)
    return high, (value - high.astype(jnp.float32)).astype(jnp.bfloat16)


def transposed_dot(left, right):
    return lax.dot_general(
        left, right, (((1,), (1,)), ((), ())), preferred_element_type=jnp.float32
    )


def select_rows(chosen, values):
    one_hot = jnp.where(chosen, 1.0, 0.0).astype(jnp.bfloat16)
    high, low = split(values)
    return jnp.dot(one_hot, high, preferred_element_type=jnp.float32) + jnp.dot(
        one_hot, low, preferred_element_type=jnp.float32
    )


def iota(shape, dimension):
    return lax.broadcasted_iota(jnp.int32, shape, dimension)


def exchange(
    records_ref,
    lists_ref,
    refs_ref,
    series_ref,
    panel_ref,
    outgoing,
    arrived,
    rows_z,
    theirs,
    send_sems,
    recv_sems,
):
    me = lax.axis_index("chan")
    lag = lax.axis_index("lag")
    segment = lax.axis_index("seg")
    core = me % CORES
    z = (me // CORES) % Z
    y = me // (CORES * Z)
    along = segment * Z + z

    def owner(y_at, z_at, core_at):
        return (y_at * Z + z_at) * CORES + core_at

    def copy(source, target, number, **device):
        return pltpu.make_async_remote_copy(
            src_ref=source,
            dst_ref=target,
            send_sem=send_sems.at[number],
            recv_sem=recv_sems.at[number],
            device_id=device,
            device_id_type=MESH,
        )

    barrier = pltpu.get_barrier_semaphore()

    def greet_owner(step, carry):
        pl.semaphore_signal(
            barrier,
            inc=1,
            device_id={"chan": (me + step) % OWNERS},
            device_id_type=MESH,
        )
        return carry

    def greet_z(step, carry):
        pl.semaphore_signal(
            barrier,
            inc=1,
            device_id={"chan": owner(y, step, core), "seg": 1 - segment},
            device_id_type=MESH,
        )
        return carry

    lax.fori_loop(1, OWNERS, greet_owner, 0)
    lax.fori_loop(0, Z, greet_z, 0)
    for step in range(1, LAG_PARTS):
        pl.semaphore_signal(
            barrier,
            inc=1,
            device_id={"lag": (lag + step) % LAG_PARTS},
            device_id_type=MESH,
        )

    own = lists_ref[pl.ds(me, 1), :]
    own_down = jnp.transpose(jnp.broadcast_to(own.astype(jnp.float32), (ROWS, ROWS)))
    own_down = own_down.astype(jnp.int32)
    own_block = own // ROWS
    behind = (own_down // ROWS == own_block) & (own_down < own)
    rank = jnp.sum(jnp.where(behind, 1, 0), axis=0, keepdims=True)
    refs = refs_ref[...].astype(jnp.float32)
    refs_down = jnp.transpose(
        jnp.broadcast_to(jnp.concatenate([refs, refs], axis=1), (ROWS, ROWS))
    )[:REF].astype(jnp.int32)
    number = iota((REF, ROWS), 0)
    holder = owner((number // Z) % Y, number % Z, number // (Y * Z))
    panel_at = jnp.sum(
        jnp.where(refs_down == own, holder * 8 + 2 * PARTS + 1, 0), axis=0, keepdims=True
    ) - 1
    series_at = own_block * 8 + rank * PARTS
    series_at = jnp.concatenate([series_at, series_at + 1], axis=1)
    panel_at = jnp.concatenate([panel_at, jnp.where(panel_at < 0, -1, panel_at + 1)], axis=1)
    place = iota((OWNERS * 8, PARTS * ROWS), 0)
    records = jnp.concatenate(
        [records_ref[pl.ds(part, ROWS, PARTS), :] for part in range(PARTS)], axis=0
    )
    chosen = (place == series_at) | (place == panel_at)
    outgoing[...] = select_rows(chosen, records).reshape(OWNERS, 8, LANES)

    pl.semaphore_wait(barrier, OWNERS - 1 + Z + LAG_PARTS - 1)

    def send_owner(step, carry):
        peer = (me + step) % OWNERS
        copy(
            outgoing.at[peer, pl.ds(0, SENT)], arrived.at[me, pl.ds(0, SENT)], 0, chan=peer
        ).start()
        return carry

    lax.fori_loop(1, OWNERS, send_owner, 0)
    arrived[me] = outgoing[me]

    lists = lists_ref[...].astype(jnp.float32)
    lists = jnp.transpose(jnp.concatenate([lists, lists], axis=0)).astype(jnp.int32)
    inside = lists // ROWS == me
    first = jnp.min(jnp.where(inside, lists, OWNERS * ROWS), axis=0, keepdims=True)
    second = jnp.max(jnp.where(inside, lists, -1), axis=0, keepdims=True)
    ids = jnp.where(iota((1, ROWS), 1) < OWNERS, first, second)
    turned = me * ROWS + (iota((ROWS, ROWS), 0) + segment * HALF) % ROWS
    placing = turned == ids

    def wait_all(source, target, number):
        waiting = copy(source, target, number, lag=(lag + 1) % LAG_PARTS)
        waiting.wait_recv()

    def wait_sent(source, number):
        copy(source, source, number, lag=(lag + 1) % LAG_PARTS).wait_send()

    several = arrived.at[pl.ds(0, OWNERS - 1), pl.ds(0, SENT)]
    wait_all(several, several, 0)

    rows_z[along] = jnp.concatenate(
        [
            jnp.sum(arrived[:, 2 * PARTS + part, :], axis=0, keepdims=True)
            for part in range(PARTS)
        ],
        axis=0,
    )

    def send_z(step, carry):
        peer = (along + step) % (SEGMENTS * Z)
        copy(
            rows_z.at[along],
            rows_z.at[along],
            1,
            chan=owner(y, peer % Z, core),
            seg=peer // Z,
        ).start()
        return carry

    lax.fori_loop(1, SEGMENTS * Z, send_z, 0)

    placed = select_rows(
        placing,
        jnp.concatenate(
            [
                jnp.concatenate(
                    [arrived[:, slot * PARTS + part, :] for slot in range(2)], axis=0
                )
                for part in range(PARTS)
            ],
            axis=1,
        ),
    )
    own_tiles = pl.ds((segment * LAG_PARTS + lag) * PARTS, PARTS)
    other_tiles = pl.ds(((1 - segment) * LAG_PARTS + lag) * PARTS, PARTS)
    for part in range(PARTS):
        theirs[part] = placed[HALF:, part * LANES : (part + 1) * LANES]
    swap = copy(theirs, series_ref.at[own_tiles], 2, seg=1 - segment)
    swap.start()
    first_tile = (segment * LAG_PARTS + lag) * PARTS
    for part in range(PARTS):
        series_ref[first_tile + part] = placed[:HALF, part * LANES : (part + 1) * LANES]
    for step in range(1, LAG_PARTS):
        copy(
            series_ref.at[own_tiles],
            series_ref.at[own_tiles],
            3,
            lag=(lag + step) % LAG_PARTS,
        ).start()

    z_rows = rows_z.at[pl.ds(0, SEGMENTS * Z - 1)]
    wait_all(z_rows, z_rows, 1)
    group = core * Y + y
    lag_tiles = pl.ds(lag * PARTS, PARTS)
    group_rows = pl.ds(pl.multiple_of(group * Z, Z), Z)
    for at in range(SEGMENTS):
        for part in range(PARTS):
            panel_ref[at, lag * PARTS + part, group_rows, :] = rows_z[
                at * Z : (at + 1) * Z, part, :
            ]
    group_tiles = panel_ref.at[:, lag_tiles, group_rows]
    for step in range(1, Y):
        copy(group_tiles, group_tiles, 4, chan=owner((y + step) % Y, z, core)).start()
    y_tiles = panel_ref.at[:, pl.ds(0, PARTS), pl.ds(0, (Y - 1) * Z)]
    wait_all(y_tiles, y_tiles, 4)
    core_rows = pl.ds(pl.multiple_of(core * Y * Z, Y * Z), Y * Z)
    core_tiles = panel_ref.at[:, lag_tiles, core_rows]
    for step in range(1, LAG_PARTS):
        copy(core_tiles, core_tiles, 5, lag=(lag + step) % LAG_PARTS).start()

    swap.wait_recv()
    for step in range(1, LAG_PARTS):
        copy(
            series_ref.at[other_tiles],
            series_ref.at[other_tiles],
            6,
            lag=(lag + step) % LAG_PARTS,
        ).start()
    x_tiles = panel_ref.at[:, pl.ds(0, (LAG_PARTS - 1) * PARTS), pl.ds(0, Y * Z)]
    wait_all(x_tiles, x_tiles, 5)
    half_panel = panel_ref.at[:, :, core_rows]
    across = copy(half_panel, half_panel, 7, chan=owner(y, z, 1 - core))
    across.start()
    six = series_ref.at[pl.ds(0, (LAG_PARTS - 1) * PARTS)]
    wait_all(six, six, 3)
    wait_all(six, six, 6)
    across.wait()
    wait_sent(several, 0)
    wait_sent(z_rows, 1)
    swap.wait_send()
    wait_sent(six, 3)
    wait_sent(y_tiles, 4)
    wait_sent(x_tiles, 5)
    wait_sent(six, 6)


def correlate(series_ref, panel_ref, out_ref, windows_high, windows_low, shifts_high, shifts_low):
    lag_width = LAGS // LAG_PARTS
    rows = series_ref.shape[1]
    groups = lag_width // COLUMN_LAGS
    start = lax.axis_index("lag") * lag_width
    per_segment = TILES // SEGMENTS
    panel = jnp.concatenate(
        [panel_ref[tile // per_segment, tile % per_segment] for tile in range(TERMS // LANES)]
        + [jnp.zeros((REF, LANES), jnp.float32)] * (TILES - TERMS // LANES),
        axis=1,
    )
    panel = pltpu.roll(panel, start, 1)
    for shift in range(COLUMN_LAGS):
        high, low = split(pltpu.roll(panel, shift, 1) if shift else panel)
        shifts_high[pl.ds(shift * REF, REF), :] = high
        shifts_low[pl.ds(shift * REF, REF), :] = low
    series = jnp.concatenate([series_ref[tile] for tile in range(TILES)], axis=1)
    for group in range(groups):
        lag = group * COLUMN_LAGS
        high, low = split(pltpu.roll(series, SAMPLES - lag, 1) if lag else series)
        windows_high[pl.ds(group * rows, rows), :] = high
        windows_low[pl.ds(group * rows, rows), :] = low
    total = (
        transposed_dot(windows_high[...], shifts_high[...])
        + transposed_dot(windows_high[...], shifts_low[...])
        + transposed_dot(windows_low[...], shifts_high[...])
    )
    width = COLUMN_LAGS * REF
    for group in range(groups):
        out_ref[:, pl.ds(group * width, width)] = total[group * rows : (group + 1) * rows] * (
            1.0 / math.sqrt(TERMS)
        )


VMEM = pl.BlockSpec(memory_space=pltpu.VMEM)


def shards(records_owned, section_list, ref_index):
    series, panel = pl.pallas_call(
        exchange,
        out_shape=[
            jax.ShapeDtypeStruct((TILES, HALF, LANES), jnp.float32),
            jax.ShapeDtypeStruct((SEGMENTS, TILES // SEGMENTS, REF, LANES), jnp.float32),
        ],
        in_specs=[VMEM] * 3,
        out_specs=[VMEM] * 2,
        scratch_shapes=[
            pltpu.VMEM((OWNERS, 8, LANES), jnp.float32),
            pltpu.VMEM((OWNERS, 8, LANES), jnp.float32),
            pltpu.VMEM((SEGMENTS * Z, PARTS, LANES), jnp.float32),
            pltpu.VMEM((PARTS, HALF, LANES), jnp.float32),
            pltpu.SemaphoreType.DMA((8,)),
            pltpu.SemaphoreType.DMA((8,)),
        ],
        compiler_params=pltpu.CompilerParams(
            collective_id=0, has_side_effects=True, vmem_limit_bytes=32 * 1024 * 1024
        ),
        name="exchange",
    )(
        records_owned.reshape(ROWS * PARTS, LANES),
        section_list.reshape(OWNERS, ROWS),
        ref_index.reshape(1, REF),
    )
    lag_width = LAGS // LAG_PARTS
    groups = lag_width // COLUMN_LAGS
    return pl.pallas_call(
        correlate,
        out_shape=jax.ShapeDtypeStruct((HALF, lag_width * REF), jnp.float32),
        in_specs=[VMEM] * 2,
        out_specs=VMEM,
        scratch_shapes=[pltpu.VMEM((groups * HALF, SAMPLES), jnp.bfloat16)] * 2
        + [pltpu.VMEM((COLUMN_LAGS * REF, SAMPLES), jnp.bfloat16)] * 2,
        compiler_params=pltpu.CompilerParams(vmem_limit_bytes=32 * 1024 * 1024),
        name="correlate",
    )(series, panel)


def solution(mesh):
    return jax.shard_map(
        shards,
        mesh=mesh,
        in_specs=(P("chan", "seg", "lag"), P(), P()),
        out_specs=P(("chan", "seg"), "lag"),
        check_vma=False,
    )
```

time: 253 us -> 55.3 us (0.22)
  the two profiles are of different devices: /device:TPU:2 before, /device:TPU:1 now
where the time goes in v2:
time: 55.3 us; the launch traced here: 55.1 us
  Pallas kernels  52.8 us (95%)
  local copies, waits for them, and re-layouts  2.32 us (4%)
    pallas_call x1, Pallas kernels, shards(): pl.pallas_call(exchange, out_shape=[jax.ShapeDtypeStruct((TILES, HALF, LA...  49.1 us
    pallas_call x1, Pallas kernels, shards(): pl.pallas_call(correlate, out_shape=jax.ShapeDtypeStruct((HALF, lag_width...  3.66 us
    unnamed x6, local copies, waits for them, and re-layouts  2.32 us

profile of v2, /device:TPU:1, one launch (start us, length us, event | category | flops | bytes accessed | tf_op | source)
XLA Modules:
  0.0 55.1 jit_solution(8263933714727678307)
XLA Ops:
  0.0 0.0 copy-start.2
  0.0 0.7 %copy-done.2 = s32[64]{0:T(128)S(1)} copy-done((s32[64]{0:T(128)S(1)}, s32[64]{0:T(128)}, u32[]{:S(2)}) %copy-start.2) | copy-done | bytes 280
  0.7 0.0 copy-start
  0.7 0.9 %copy-done = f32[128,1,256]{2,1,0:T(1,128)S(1)} copy-done((f32[128,1,256]{2,1,0:T(1,128)S(1)}, f32[128,1,256]{2,1,0:T(1,128)}, u32[]{:S(2)}) %copy-start) | copy-done | bytes 131096
  1.6 0.0 copy-start.1
  1.6 0.8 %copy-done.1 = s32[8192]{0:T(1024)S(1)} copy-done((s32[8192]{0:T(1024)S(1)}, s32[8192]{0:T(1024)}, u32[]{:S(2)}) %copy-start.1) | copy-done | bytes 32792
  2.3 49.1 %exchange.1 = (f32[16,64,128]{2,1,0:T(8,128)S(1)}, f32[2,8,64,128]{3,2,1,0:T(8,128)S(1)}) custom-call(f32[256,128]{1,0:T(8,128)S(1)} %bitcast.3, s32[64,128]{1,0:T(8,128)S(1)} %bitcast.4, s32[1,64]{1,0:T(1,128)S(1)} %bitcast.5), custom_call_target="tpu_custom_call" | custom-call | tf_op jit(solution)/shard_map/exchange/pallas_call | solution.py:305
  51.4 3.7 %correlate.1 = f32[64,2048]{1,0:T(8,128)} custom-call(f32[16,64,128]{2,1,0:T(8,128)S(1)} %get-tuple-element.7.series_ref, f32[2,8,64,128]{3,2,1,0:T(8,128)S(1)} %get-tuple-element.8.panel_ref), custom_call_target="tpu_custom_call" | custom-call | tf_op jit(solution)/shard_map/correlate/pallas_call | solution.py:332
Async XLA Ops:
  0.0 0.7 %copy-start.2 = (s32[64]{0:T(128)S(1)}, s32[64]{0:T(128)}, u32[]{:S(2)}) copy-start(s32[64]{0:T(128)} %param.5) | copy-start | bytes 772
  0.7 0.9 %copy-start = (f32[128,1,256]{2,1,0:T(1,128)S(1)}, f32[128,1,256]{2,1,0:T(1,128)}, u32[]{:S(2)}) copy-start(f32[128,1,256]{2,1,0:T(1,128)} %param.3) | copy-start | bytes 393220
  1.6 0.8 %copy-start.1 = (s32[8192]{0:T(1024)S(1)}, s32[8192]{0:T(1024)}, u32[]{:S(2)}) copy-start(s32[8192]{0:T(1024)} %param.4) | copy-start | bytes 98308

commit v3 on v2

v3 whole, which is shorter than its diff:
```python
import math

import jax
import jax.numpy as jnp
from jax import lax
from jax.experimental import pallas as pl
from jax.experimental.pallas import tpu as pltpu
from jax.sharding import PartitionSpec as P

MESH = pl.DeviceIdType.MESH
LAGS = 128
SAMPLES = 2048
REF = 64
TERMS = SAMPLES - LAGS
LANES = 128
TILES = SAMPLES // LANES
COLUMN_LAGS = 4
OWNERS = 64
ROWS = 128
HALF = 64
SEGMENTS = 2
LAG_PARTS = 4
Y, Z, CORES = 4, 8, 2
PARTS = 2


def split(value):
    high = value.astype(jnp.bfloat16)
    return high, (value - high.astype(jnp.float32)).astype(jnp.bfloat16)


def transposed_dot(left, right):
    return lax.dot_general(
        left, right, (((1,), (1,)), ((), ())), preferred_element_type=jnp.float32
    )


def select_rows(chosen, values):
    one_hot = jnp.where(chosen, 1.0, 0.0).astype(jnp.bfloat16)
    high, low = split(values)
    return jnp.dot(one_hot, high, preferred_element_type=jnp.float32) + jnp.dot(
        one_hot, low, preferred_element_type=jnp.float32
    )


def iota(shape, dimension):
    return lax.broadcasted_iota(jnp.int32, shape, dimension)


def exchange(
    records_hbm,
    lists_hbm,
    refs_hbm,
    series_ref,
    panel_ref,
    records_ref,
    lists_ref,
    refs_ref,
    outgoing,
    arrived,
    rows_z,
    theirs,
    load_sems,
    send_sems,
    recv_sems,
):
    me = lax.axis_index("chan")
    lag = lax.axis_index("lag")
    segment = lax.axis_index("seg")
    core = me % CORES
    z = (me // CORES) % Z
    y = me // (CORES * Z)
    along = segment * Z + z

    def owner(y_at, z_at, core_at):
        return (y_at * Z + z_at) * CORES + core_at

    def copy(source, target, number, **device):
        return pltpu.make_async_remote_copy(
            src_ref=source,
            dst_ref=target,
            send_sem=send_sems.at[number],
            recv_sem=recv_sems.at[number],
            device_id=device,
            device_id_type=MESH,
        )

    def greet(**device):
        pl.semaphore_signal(barrier, inc=1, device_id=device, device_id_type=MESH)

    def wait_all(block, number):
        copy(block, block, number, lag=(lag + 1) % LAG_PARTS).wait_recv()

    def wait_sent(block, number):
        copy(block, block, number, lag=(lag + 1) % LAG_PARTS).wait_send()

    barrier = pltpu.get_barrier_semaphore()

    def greet_owner(step, carry):
        greet(chan=(me + step) % OWNERS)
        return carry

    def greet_z(step, carry):
        greet(chan=owner(y, step, core), seg=1 - segment)
        return carry

    loads = [
        pltpu.make_async_copy(source, target, load_sems.at[number])
        for number, (source, target) in enumerate(
            [(records_hbm, records_ref), (lists_hbm, lists_ref), (refs_hbm, refs_ref)]
        )
    ]
    for load in loads:
        load.start()
    lax.fori_loop(1, OWNERS, greet_owner, 0)
    lax.fori_loop(0, Z, greet_z, 0)
    for y_step in range(Y):
        for step in range(1, LAG_PARTS):
            greet(chan=owner((y + y_step) % Y, z, core), lag=(lag + step) % LAG_PARTS)
    for load in loads:
        load.wait()

    own = lists_ref[pl.ds(me, 1), :]
    own_down = jnp.transpose(jnp.broadcast_to(own.astype(jnp.float32), (ROWS, ROWS)))
    own_down = own_down.astype(jnp.int32)
    own_block = own // ROWS
    behind = (own_down // ROWS == own_block) & (own_down < own)
    rank = jnp.sum(jnp.where(behind, 1, 0), axis=0, keepdims=True)
    refs = refs_ref[...].astype(jnp.float32)
    refs_down = jnp.transpose(
        jnp.broadcast_to(jnp.concatenate([refs, refs], axis=1), (ROWS, ROWS))
    )[:REF].astype(jnp.int32)
    number = iota((REF, ROWS), 0)
    holder = owner((number // Z) % Y, number % Z, number // (Y * Z))
    panel_at = (
        jnp.sum(jnp.where(refs_down == own, holder * 8 + 1, 0), axis=0, keepdims=True) - 1
    )
    series_at = own_block * 8 + PARTS + rank
    series_at = jnp.concatenate([series_at, series_at + 2], axis=1)
    panel_at = jnp.concatenate([panel_at, jnp.where(panel_at < 0, -1, panel_at + 1)], axis=1)
    place = iota((OWNERS * 8, PARTS * ROWS), 0)
    records = jnp.concatenate(
        [records_ref[pl.ds(part, ROWS, PARTS), :] for part in range(PARTS)], axis=0
    )
    chosen = (place == series_at) | (place == panel_at)
    outgoing[...] = select_rows(chosen, records).reshape(OWNERS, 8, LANES)

    pl.semaphore_wait(barrier, OWNERS - 1 + Z + Y * (LAG_PARTS - 1))

    for stage in range(1 + PARTS):

        def send_owner(step, carry, pair=pl.ds(2 * stage, 2), stage=stage):
            peer = (me + step) % OWNERS
            copy(outgoing.at[peer, pair], arrived.at[me, pair], stage, chan=peer).start()
            return carry

        lax.fori_loop(1, OWNERS, send_owner, 0)
    arrived[me] = outgoing[me]

    lists = lists_ref[...].astype(jnp.float32)
    lists = jnp.transpose(jnp.concatenate([lists, lists], axis=0)).astype(jnp.int32)
    inside = lists // ROWS == me
    first = jnp.min(jnp.where(inside, lists, OWNERS * ROWS), axis=0, keepdims=True)
    second = jnp.max(jnp.where(inside, lists, -1), axis=0, keepdims=True)
    ids = jnp.where(iota((1, ROWS), 1) < OWNERS, first, second)
    turned = me * ROWS + (iota((ROWS, ROWS), 0) + segment * HALF) % ROWS
    placing = turned == ids
    pairs = [arrived.at[pl.ds(0, OWNERS - 1), pl.ds(2 * stage, 2)] for stage in range(1 + PARTS)]

    wait_all(pairs[0], 0)
    rows_z[along] = jnp.concatenate(
        [jnp.sum(arrived[:, part, :], axis=0, keepdims=True) for part in range(PARTS)], axis=0
    )

    def send_z(step, carry):
        peer = (along + step) % (SEGMENTS * Z)
        copy(
            rows_z.at[along],
            rows_z.at[along],
            3,
            chan=owner(y, peer % Z, core),
            seg=peer // Z,
        ).start()
        return carry

    lax.fori_loop(1, SEGMENTS * Z, send_z, 0)

    own_tile = (segment * LAG_PARTS + lag) * PARTS
    other_tile = ((1 - segment) * LAG_PARTS + lag) * PARTS
    swaps = [
        copy(theirs.at[part], series_ref.at[own_tile + part], 6 + part, seg=1 - segment)
        for part in range(PARTS)
    ]

    def forward(tile, number):
        for step in range(1, LAG_PARTS):
            copy(
                series_ref.at[tile], series_ref.at[tile], number, lag=(lag + step) % LAG_PARTS
            ).start()

    def place_part(part):
        wait_all(pairs[1 + part], 1 + part)
        placed = select_rows(
            placing,
            jnp.concatenate(
                [arrived[:, PARTS * (1 + part) + slot, :] for slot in range(2)], axis=0
            ),
        )
        theirs[part] = placed[HALF:]
        swaps[part].start()
        series_ref[own_tile + part] = placed[:HALF]
        forward(own_tile + part, 8 + part)

    place_part(0)

    z_rows = rows_z.at[pl.ds(0, SEGMENTS * Z - 1)]
    wait_all(z_rows, 3)
    lag_tiles = pl.ds(lag * PARTS, PARTS)
    group_rows = pl.ds(pl.multiple_of((core * Y + y) * Z, Z), Z)
    for at in range(SEGMENTS):
        for part in range(PARTS):
            panel_ref[at, lag * PARTS + part, group_rows, :] = rows_z[
                at * Z : (at + 1) * Z, part, :
            ]
    group_tiles = panel_ref.at[:, lag_tiles, group_rows]
    for y_step in range(Y):
        for step in range(LAG_PARTS):
            if y_step or step:
                copy(
                    group_tiles,
                    group_tiles,
                    4,
                    chan=owner((y + y_step) % Y, z, core),
                    lag=(lag + step) % LAG_PARTS,
                ).start()

    place_part(1)
    for part in range(PARTS):
        swaps[part].wait_recv()
        forward(other_tile + part, 10 + part)

    xy_tiles = panel_ref.at[:, pl.ds(0, 5), pl.ds(0, 6 * Z)]
    wait_all(xy_tiles, 4)
    core_rows = pl.ds(pl.multiple_of(core * Y * Z, Y * Z), Y * Z)
    half_panel = panel_ref.at[:, :, core_rows]
    across = copy(half_panel, half_panel, 5, chan=owner(y, z, 1 - core))
    across.start()
    three = series_ref.at[pl.ds(0, LAG_PARTS - 1)]
    for number in range(8, 12):
        wait_all(three, number)
    across.wait()
    for stage in range(1 + PARTS):
        wait_sent(pairs[stage], stage)
    wait_sent(z_rows, 3)
    wait_sent(xy_tiles, 4)
    for part in range(PARTS):
        swaps[part].wait_send()
    for number in range(8, 12):
        wait_sent(three, number)


def correlate(series_ref, panel_ref, out_ref, windows_high, windows_low, shifts_high, shifts_low):
    lag_width = LAGS // LAG_PARTS
    rows = series_ref.shape[1]
    groups = lag_width // COLUMN_LAGS
    start = lax.axis_index("lag") * lag_width
    per_segment = TILES // SEGMENTS
    panel = jnp.concatenate(
        [panel_ref[tile // per_segment, tile % per_segment] for tile in range(TERMS // LANES)]
        + [jnp.zeros((REF, LANES), jnp.float32)] * (TILES - TERMS // LANES),
        axis=1,
    )
    panel = pltpu.roll(panel, start, 1)
    for shift in range(COLUMN_LAGS):
        high, low = split(pltpu.roll(panel, shift, 1) if shift else panel)
        shifts_high[pl.ds(shift * REF, REF), :] = high
        shifts_low[pl.ds(shift * REF, REF), :] = low
    series = jnp.concatenate([series_ref[tile] for tile in range(TILES)], axis=1)
    for group in range(groups):
        lag = group * COLUMN_LAGS
        high, low = split(pltpu.roll(series, SAMPLES - lag, 1) if lag else series)
        windows_high[pl.ds(group * rows, rows), :] = high
        windows_low[pl.ds(group * rows, rows), :] = low
    total = (
        transposed_dot(windows_high[...], shifts_high[...])
        + transposed_dot(windows_high[...], shifts_low[...])
        + transposed_dot(windows_low[...], shifts_high[...])
    )
    width = COLUMN_LAGS * REF
    for group in range(groups):
        out_ref[:, pl.ds(group * width, width)] = total[group * rows : (group + 1) * rows] * (
            1.0 / math.sqrt(TERMS)
        )


VMEM = pl.BlockSpec(memory_space=pltpu.VMEM)


def shards(records_owned, section_list, ref_index):
    series, panel = pl.pallas_call(
        exchange,
        out_shape=[
            jax.ShapeDtypeStruct((TILES, HALF, LANES), jnp.float32),
            jax.ShapeDtypeStruct((SEGMENTS, TILES // SEGMENTS, REF, LANES), jnp.float32),
        ],
        in_specs=[pl.BlockSpec(memory_space=pltpu.HBM)] * 3,
        out_specs=[VMEM] * 2,
        scratch_shapes=[
            pltpu.VMEM((ROWS * PARTS, LANES), jnp.float32),
            pltpu.VMEM((OWNERS, ROWS), jnp.int32),
            pltpu.VMEM((1, REF), jnp.int32),
            pltpu.VMEM((OWNERS, 8, LANES), jnp.float32),
            pltpu.VMEM((OWNERS, 8, LANES), jnp.float32),
            pltpu.VMEM((SEGMENTS * Z, PARTS, LANES), jnp.float32),
            pltpu.VMEM((PARTS, HALF, LANES), jnp.float32),
            pltpu.SemaphoreType.DMA((3,)),
            pltpu.SemaphoreType.DMA((12,)),
            pltpu.SemaphoreType.DMA((12,)),
        ],
        compiler_params=pltpu.CompilerParams(
            collective_id=0, has_side_effects=True, vmem_limit_bytes=32 * 1024 * 1024
        ),
        name="exchange",
    )(
        *[
            pltpu.with_memory_space_constraint(value, pltpu.HBM)
            for value in (
                records_owned.reshape(ROWS * PARTS, LANES),
                section_list.reshape(OWNERS, ROWS),
                ref_index.reshape(1, REF),
            )
        ]
    )
    lag_width = LAGS // LAG_PARTS
    groups = lag_width // COLUMN_LAGS
    return pl.pallas_call(
        correlate,
        out_shape=jax.ShapeDtypeStruct((HALF, lag_width * REF), jnp.float32),
        in_specs=[VMEM] * 2,
        out_specs=VMEM,
        scratch_shapes=[pltpu.VMEM((groups * HALF, SAMPLES), jnp.bfloat16)] * 2
        + [pltpu.VMEM((COLUMN_LAGS * REF, SAMPLES), jnp.bfloat16)] * 2,
        compiler_params=pltpu.CompilerParams(vmem_limit_bytes=32 * 1024 * 1024),
        name="correlate",
    )(series, panel)


def solution(mesh):
    return jax.shard_map(
        shards,
        mesh=mesh,
        in_specs=(P("chan", "seg", "lag"), P(), P()),
        out_specs=P(("chan", "seg"), "lag"),
        check_vma=False,
    )
```

time: 55.3 us -> 50 us (0.904)
  Pallas kernels: 52.8 us -> 49.9 us
  local copies, waits for them, and re-layouts: 2.32 us -> 0 us
    pallas_call x1, Pallas kernels: 49.1 us -> 46.3 us  [shards(): pl.pallas_call(exchange, out_shape=[jax.ShapeDtypeStruct((TILES, HALF, LA...]
    unnamed x6 -> x0, local copies, waits for them, and re-layouts: 2.32 us -> none
where the time goes in v3:
time: 50 us; the launch traced here: 49.9 us
  Pallas kernels  49.9 us (100%)
    pallas_call x1, Pallas kernels, shards(): pl.pallas_call(exchange, out_shape=[jax.ShapeDtypeStruct((TILES, HALF, LA...  46.3 us
    pallas_call x1, Pallas kernels, shards(): pl.pallas_call(correlate, out_shape=jax.ShapeDtypeStruct((HALF, lag_width...  3.65 us

profile of v3, /device:TPU:1, one launch (start us, length us, event | category | flops | bytes accessed | tf_op | source)
XLA Modules:
  0.0 49.9 jit_solution(14753622444795210994)
XLA Ops:
  0.0 46.3 %exchange.1 = (f32[16,64,128]{2,1,0:T(8,128)S(1)}, f32[2,8,64,128]{3,2,1,0:T(8,128)S(1)}) custom-call(f32[256,128]{1,0:T(8,128)} %bitcast.3, s32[64,128]{1,0:T(8,128)} %bitcast.4, s32[1,64]{1,0:T(1,128)} %bitcast.5), custom_call_target="tpu_custom_call" | custom-call | tf_op jit(solution)/shard_map/exchange/pallas_call | solution.py:300
  46.3 3.6 %correlate.1 = f32[64,2048]{1,0:T(8,128)} custom-call(f32[16,64,128]{2,1,0:T(8,128)S(1)} %get-tuple-element.7.series_ref, f32[2,8,64,128]{3,2,1,0:T(8,128)S(1)} %get-tuple-element.8.panel_ref), custom_call_target="tpu_custom_call" | custom-call | tf_op jit(solution)/shard_map/correlate/pallas_call | solution.py:336

commit v4 on v3

--- a/solution.py
+++ b/solution.py
@@ -21,6 +21,7 @@
 SEGMENTS = 2
 LAG_PARTS = 4
 Y, Z, CORES = 4, 8, 2
+WIDE = Y * CORES
 PARTS = 2
 
 
@@ -57,7 +58,11 @@
     lists_ref,
     refs_ref,
     outgoing,
-    arrived,
+    across_plane,
+    line_out,
+    along_line,
+    sums_out,
+    sums_in,
     rows_z,
     theirs,
     load_sems,
@@ -75,6 +80,16 @@
     def owner(y_at, z_at, core_at):
         return (y_at * Z + z_at) * CORES + core_at
 
+    wide = y * CORES + core
+
+    def plane_peer(step):
+        at = (wide + step) % WIDE
+        return owner(at // CORES, z, at % CORES)
+
+    def line_peer(step):
+        at = (along + step) % (SEGMENTS * Z)
+        return {"chan": owner(y, at % Z, core), "seg": at // Z}
+
     def copy(source, target, number, **device):
         return pltpu.make_async_remote_copy(
             src_ref=source,
@@ -96,14 +111,6 @@
 
     barrier = pltpu.get_barrier_semaphore()
 
-    def greet_owner(step, carry):
-        greet(chan=(me + step) % OWNERS)
-        return carry
-
-    def greet_z(step, carry):
-        greet(chan=owner(y, step, core), seg=1 - segment)
-        return carry
-
     loads = [
         pltpu.make_async_copy(source, target, load_sems.at[number])
         for number, (source, target) in enumerate(
@@ -112,8 +119,10 @@
     ]
     for load in loads:
         load.start()
-    lax.fori_loop(1, OWNERS, greet_owner, 0)
-    lax.fori_loop(0, Z, greet_z, 0)
+    for step in range(1, WIDE):
+        greet(chan=plane_peer(step))
+    for step in range(1, SEGMENTS * Z):
+        greet(**line_peer(step))
     for y_step in range(Y):
         for step in range(1, LAG_PARTS):
             greet(chan=owner((y + y_step) % Y, z, core), lag=(lag + step) % LAG_PARTS)
@@ -131,31 +140,35 @@
         jnp.broadcast_to(jnp.concatenate([refs, refs], axis=1), (ROWS, ROWS))
     )[:REF].astype(jnp.int32)
     number = iota((REF, ROWS), 0)
-    holder = owner((number // Z) % Y, number % Z, number // (Y * Z))
+    number = number // (Y * Z) + (number // Z) % Y * CORES, number % Z
     panel_at = (
-        jnp.sum(jnp.where(refs_down == own, holder * 8 + 1, 0), axis=0, keepdims=True) - 1
-    )
-    series_at = own_block * 8 + PARTS + rank
-    series_at = jnp.concatenate([series_at, series_at + 2], axis=1)
+        jnp.sum(
+            jnp.where(refs_down == own, (number[0] * Z + number[1]) * 2 + 1, 0),
+            axis=0,
+            keepdims=True,
+        )
+        - 1
+    )
+    own_wide = own_block // (Z * CORES) * CORES + own_block % CORES
+    series_at = (own_wide * Z + own_block // CORES % Z) * 2 + rank
+    series_at = jnp.concatenate([series_at + ROWS, series_at + 2 * ROWS], axis=1)
     panel_at = jnp.concatenate([panel_at, jnp.where(panel_at < 0, -1, panel_at + 1)], axis=1)
-    place = iota((OWNERS * 8, PARTS * ROWS), 0)
+    place = iota(((1 + PARTS) * ROWS, PARTS * ROWS), 0)
     records = jnp.concatenate(
         [records_ref[pl.ds(part, ROWS, PARTS), :] for part in range(PARTS)], axis=0
     )
     chosen = (place == series_at) | (place == panel_at)
-    outgoing[...] = select_rows(chosen, records).reshape(OWNERS, 8, LANES)
-
-    pl.semaphore_wait(barrier, OWNERS - 1 + Z + Y * (LAG_PARTS - 1))
-
-    for stage in range(1 + PARTS):
-
-        def send_owner(step, carry, pair=pl.ds(2 * stage, 2), stage=stage):
-            peer = (me + step) % OWNERS
-            copy(outgoing.at[peer, pair], arrived.at[me, pair], stage, chan=peer).start()
-            return carry
-
-        lax.fori_loop(1, OWNERS, send_owner, 0)
-    arrived[me] = outgoing[me]
+    outgoing[...] = select_rows(chosen, records).reshape(1 + PARTS, WIDE, 2 * Z, LANES)
+
+    pl.semaphore_wait(barrier, WIDE - 1 + SEGMENTS * Z - 1 + Y * (LAG_PARTS - 1))
+
+    for kind in range(1 + PARTS):
+        for step in range(1, WIDE):
+            at = (wide + step) % WIDE
+            copy(
+                outgoing.at[kind, at], across_plane.at[kind, wide], kind, chan=plane_peer(step)
+            ).start()
+        across_plane[kind, wide] = outgoing[kind, wide]
 
     lists = lists_ref[...].astype(jnp.float32)
     lists = jnp.transpose(jnp.concatenate([lists, lists], axis=0)).astype(jnp.int32)
@@ -164,31 +177,57 @@
     second = jnp.max(jnp.where(inside, lists, -1), axis=0, keepdims=True)
     ids = jnp.where(iota((1, ROWS), 1) < OWNERS, first, second)
     turned = me * ROWS + (iota((ROWS, ROWS), 0) + segment * HALF) % ROWS
-    placing = turned == ids
-    pairs = [arrived.at[pl.ds(0, OWNERS - 1), pl.ds(2 * stage, 2)] for stage in range(1 + PARTS)]
-
-    wait_all(pairs[0], 0)
-    rows_z[along] = jnp.concatenate(
-        [jnp.sum(arrived[:, part, :], axis=0, keepdims=True) for part in range(PARTS)], axis=0
-    )
-
-    def send_z(step, carry):
-        peer = (along + step) % (SEGMENTS * Z)
-        copy(
-            rows_z.at[along],
-            rows_z.at[along],
-            3,
-            chan=owner(y, peer % Z, core),
-            seg=peer // Z,
-        ).start()
-        return carry
-
-    lax.fori_loop(1, SEGMENTS * Z, send_z, 0)
+    down, right = iota((ROWS, ROWS), 0), iota((ROWS, ROWS), 1)
+    right_wide = right // 2 % WIDE
+    right_owner = owner(right_wide // CORES, right // (2 * WIDE), right_wide % CORES)
+    reorder = jnp.where(down == right % 2 * OWNERS + right_owner, 1.0, 0.0).astype(jnp.bfloat16)
+    placing = (
+        jnp.dot(
+            jnp.where(turned == ids, 1.0, 0.0).astype(jnp.bfloat16),
+            reorder,
+            preferred_element_type=jnp.float32,
+        )
+        > 0.5
+    )
+    by_line = right == (down // 2 % WIDE * Z + down // (2 * WIDE)) * 2 + down % 2
+
+    seven_plane = [across_plane.at[kind, pl.ds(0, WIDE - 1)] for kind in range(1 + PARTS)]
+    seven_line = along_line.at[0, pl.ds(0, Z - 1)]
+
+    wait_all(seven_plane[0], 0)
+    sums = jnp.sum(across_plane[0], axis=0)
+    for at in range(Z):
+        sums_out[at] = sums[2 * at : 2 * at + 2]
+    for step in range(1, Z):
+        at = (z + step) % Z
+        copy(sums_out.at[at], sums_in.at[z], 3, chan=owner(y, at, core)).start()
+    sums_in[z] = sums_out[z]
+
+    def send_line(part):
+        wait_all(seven_plane[1 + part], 1 + part)
+        line_out[part] = select_rows(
+            by_line, across_plane[1 + part].reshape(ROWS, LANES)
+        ).reshape(Z, 2 * WIDE, LANES)
+        for step in range(1, Z):
+            at = (z + step) % Z
+            copy(
+                line_out.at[part, at], along_line.at[part, z], 4 + part, chan=owner(y, at, core)
+            ).start()
+        along_line[part, z] = line_out[part, z]
+
+    send_line(0)
+    send_line(1)
+
+    seven_sums = sums_in.at[pl.ds(0, Z - 1)]
+    wait_all(seven_sums, 3)
+    rows_z[along] = jnp.sum(sums_in[...], axis=0)
+    for step in range(1, SEGMENTS * Z):
+        copy(rows_z.at[along], rows_z.at[along], 6, **line_peer(step)).start()
 
     own_tile = (segment * LAG_PARTS + lag) * PARTS
     other_tile = ((1 - segment) * LAG_PARTS + lag) * PARTS
     swaps = [
-        copy(theirs.at[part], series_ref.at[own_tile + part], 6 + part, seg=1 - segment)
+        copy(theirs.at[part], series_ref.at[own_tile + part], 9 + part, seg=1 - segment)
         for part in range(PARTS)
     ]
 
@@ -199,22 +238,21 @@
             ).start()
 
     def place_part(part):
-        wait_all(pairs[1 + part], 1 + part)
-        placed = select_rows(
-            placing,
-            jnp.concatenate(
-                [arrived[:, PARTS * (1 + part) + slot, :] for slot in range(2)], axis=0
-            ),
-        )
+        wait_all(seven_line, 4 + part)
+        placed = select_rows(placing, along_line[part].reshape(ROWS, LANES))
         theirs[part] = placed[HALF:]
-        swaps[part].start()
+
+        @pl.when(segment == 1)
+        def _():
+            swaps[part].start()
+
         series_ref[own_tile + part] = placed[:HALF]
-        forward(own_tile + part, 8 + part)
+        forward(own_tile + part, 11 + part)
 
     place_part(0)
 
     z_rows = rows_z.at[pl.ds(0, SEGMENTS * Z - 1)]
-    wait_all(z_rows, 3)
+    wait_all(z_rows, 6)
     lag_tiles = pl.ds(lag * PARTS, PARTS)
     group_rows = pl.ds(pl.multiple_of((core * Y + y) * Z, Z), Z)
     for at in range(SEGMENTS):
@@ -229,7 +267,7 @@
                 copy(
                     group_tiles,
                     group_tiles,
-                    4,
+                    7,
                     chan=owner((y + y_step) % Y, z, core),
                     lag=(lag + step) % LAG_PARTS,
                 ).start()
@@ -237,25 +275,32 @@
     place_part(1)
     for part in range(PARTS):
         swaps[part].wait_recv()
-        forward(other_tile + part, 10 + part)
+        forward(other_tile + part, 13 + part)
+
+    @pl.when(segment == 0)
+    def _():
+        for part in range(PARTS):
+            swaps[part].start()
 
     xy_tiles = panel_ref.at[:, pl.ds(0, 5), pl.ds(0, 6 * Z)]
-    wait_all(xy_tiles, 4)
+    wait_all(xy_tiles, 7)
     core_rows = pl.ds(pl.multiple_of(core * Y * Z, Y * Z), Y * Z)
     half_panel = panel_ref.at[:, :, core_rows]
-    across = copy(half_panel, half_panel, 5, chan=owner(y, z, 1 - core))
+    across = copy(half_panel, half_panel, 8, chan=owner(y, z, 1 - core))
     across.start()
     three = series_ref.at[pl.ds(0, LAG_PARTS - 1)]
-    for number in range(8, 12):
+    for number in range(11, 15):
         wait_all(three, number)
     across.wait()
-    for stage in range(1 + PARTS):
-        wait_sent(pairs[stage], stage)
-    wait_sent(z_rows, 3)
-    wait_sent(xy_tiles, 4)
+    for kind in range(1 + PARTS):
+        wait_sent(seven_plane[kind], kind)
+    wait_sent(seven_sums, 3)
     for part in range(PARTS):
+        wait_sent(seven_line, 4 + part)
         swaps[part].wait_send()
-    for number in range(8, 12):
+    wait_sent(z_rows, 6)
+    wait_sent(xy_tiles, 7)
+    for number in range(11, 15):
         wait_sent(three, number)
 
 
@@ -309,13 +354,17 @@
             pltpu.VMEM((ROWS * PARTS, LANES), jnp.float32),
             pltpu.VMEM((OWNERS, ROWS), jnp.int32),
             pltpu.VMEM((1, REF), jnp.int32),
-            pltpu.VMEM((OWNERS, 8, LANES), jnp.float32),
-            pltpu.VMEM((OWNERS, 8, LANES), jnp.float32),
+            pltpu.VMEM((1 + PARTS, WIDE, 2 * Z, LANES), jnp.float32),
+            pltpu.VMEM((1 + PARTS, WIDE, 2 * Z, LANES), jnp.float32),
+            pltpu.VMEM((PARTS, Z, 2 * WIDE, LANES), jnp.float32),
+            pltpu.VMEM((PARTS, Z, 2 * WIDE, LANES), jnp.float32),
+            pltpu.VMEM((Z, PARTS, LANES), jnp.float32),
+            pltpu.VMEM((Z, PARTS, LANES), jnp.float32),
             pltpu.VMEM((SEGMENTS * Z, PARTS, LANES), jnp.float32),
             pltpu.VMEM((PARTS, HALF, LANES), jnp.float32),
             pltpu.SemaphoreType.DMA((3,)),
-            pltpu.SemaphoreType.DMA((12,)),
-            pltpu.SemaphoreType.DMA((12,)),
+            pltpu.SemaphoreType.DMA((15,)),
+            pltpu.SemaphoreType.DMA((15,)),
         ],
         compiler_params=pltpu.CompilerParams(
             collective_id=0, has_side_effects=True, vmem_limit_bytes=32 * 1024 * 1024

time: 50 us -> 53.3 us (1.066)
  the two profiles are of different devices: /device:TPU:1 before, /device:TPU:448 now
where the time goes in v4:
time: 53.3 us; the launch traced here: 53.2 us
  Pallas kernels  53.2 us (100%)
    pallas_call x1, Pallas kernels, shards(): pl.pallas_call(exchange, out_shape=[jax.ShapeDtypeStruct((TILES, HALF, LA...  49.5 us
    pallas_call x1, Pallas kernels, shards(): pl.pallas_call(correlate, out_shape=jax.ShapeDtypeStruct((HALF, lag_width...  3.65 us

profile of v4, /device:TPU:448, one launch (start us, length us, event | category | flops | bytes accessed | tf_op | source)
XLA Modules:
  0.0 53.2 jit_solution(15326957724306858016)
XLA Ops:
  0.0 49.5 %exchange.1 = (f32[16,64,128]{2,1,0:T(8,128)S(1)}, f32[2,8,64,128]{3,2,1,0:T(8,128)S(1)}) custom-call(f32[256,128]{1,0:T(8,128)} %bitcast.3, s32[64,128]{1,0:T(8,128)} %bitcast.4, s32[1,64]{1,0:T(1,128)} %bitcast.5), custom_call_target="tpu_custom_call" | custom-call | tf_op jit(solution)/shard_map/exchange/pallas_call | solution.py:345
  49.5 3.7 %correlate.1 = f32[64,2048]{1,0:T(8,128)} custom-call(f32[16,64,128]{2,1,0:T(8,128)S(1)} %get-tuple-element.7.series_ref, f32[2,8,64,128]{3,2,1,0:T(8,128)S(1)} %get-tuple-element.8.panel_ref), custom_call_target="tpu_custom_call" | custom-call | tf_op jit(solution)/shard_map/correlate/pallas_call | solution.py:385

commit v5 on v4

--- a/solution.py
+++ b/solution.py
@@ -22,6 +22,8 @@
 LAG_PARTS = 4
 Y, Z, CORES = 4, 8, 2
 WIDE = Y * CORES
+NEAR = 2
+KEPT = Z // NEAR
 PARTS = 2
 
 
@@ -57,14 +59,15 @@
     records_ref,
     lists_ref,
     refs_ref,
+    panel_out,
+    panel_in,
     outgoing,
     across_plane,
     line_out,
     along_line,
-    sums_out,
-    sums_in,
-    rows_z,
+    sums,
     theirs,
+    late_sem,
     load_sems,
     send_sems,
     recv_sems,
@@ -86,9 +89,13 @@
         at = (wide + step) % WIDE
         return owner(at // CORES, z, at % CORES)
 
-    def line_peer(step):
-        at = (along + step) % (SEGMENTS * Z)
-        return {"chan": owner(y, at % Z, core), "seg": at // Z}
+    first_near = z // NEAR * NEAR
+    near = wide * NEAR + z % NEAR
+
+    def near_peer(step):
+        at = (near + step) % (WIDE * NEAR)
+        at_wide = at // NEAR
+        return at, owner(at_wide // CORES, first_near + at % NEAR, at_wide % CORES)
 
     def copy(source, target, number, **device):
         return pltpu.make_async_remote_copy(
@@ -119,10 +126,17 @@
     ]
     for load in loads:
         load.start()
-    for step in range(1, WIDE):
-        greet(chan=plane_peer(step))
-    for step in range(1, SEGMENTS * Z):
-        greet(**line_peer(step))
+
+    @pl.when(segment == 0)
+    def _():
+        for step in range(Z):
+            greet(chan=owner(y, step, core), seg=1)
+
+    for step in range(1, WIDE * NEAR):
+        greet(chan=near_peer(step)[1])
+    for step in range(1, Z // NEAR):
+        for at in range(NEAR):
+            greet(chan=owner(y, (first_near + step * NEAR + at) % Z, core))
     for y_step in range(Y):
         for step in range(1, LAG_PARTS):
             greet(chan=owner((y + y_step) % Y, z, core), lag=(lag + step) % LAG_PARTS)
@@ -140,35 +154,51 @@
         jnp.broadcast_to(jnp.concatenate([refs, refs], axis=1), (ROWS, ROWS))
     )[:REF].astype(jnp.int32)
     number = iota((REF, ROWS), 0)
-    number = number // (Y * Z) + (number // Z) % Y * CORES, number % Z
-    panel_at = (
-        jnp.sum(
-            jnp.where(refs_down == own, (number[0] * Z + number[1]) * 2 + 1, 0),
-            axis=0,
-            keepdims=True,
-        )
-        - 1
-    )
+    target = (number // (Y * Z) + (number // Z) % Y * CORES) * NEAR + number % Z // KEPT
+    panel_at = jnp.sum(
+        jnp.where(refs_down == own, target * 8 + number % KEPT + 1, 0), axis=0, keepdims=True
+    )
+    panel_at = panel_at - 1
     own_wide = own_block // (Z * CORES) * CORES + own_block % CORES
     series_at = (own_wide * Z + own_block // CORES % Z) * 2 + rank
-    series_at = jnp.concatenate([series_at + ROWS, series_at + 2 * ROWS], axis=1)
-    panel_at = jnp.concatenate([panel_at, jnp.where(panel_at < 0, -1, panel_at + 1)], axis=1)
-    place = iota(((1 + PARTS) * ROWS, PARTS * ROWS), 0)
+    series_at = jnp.concatenate([series_at, series_at + ROWS], axis=1)
+    panel_at = jnp.concatenate([panel_at, jnp.where(panel_at < 0, -1, panel_at + KEPT)], axis=1)
+    place = iota((PARTS * ROWS, PARTS * ROWS), 0)
+    panel_place = iota((WIDE * NEAR * 8, PARTS * ROWS), 0)
     records = jnp.concatenate(
         [records_ref[pl.ds(part, ROWS, PARTS), :] for part in range(PARTS)], axis=0
     )
-    chosen = (place == series_at) | (place == panel_at)
-    outgoing[...] = select_rows(chosen, records).reshape(1 + PARTS, WIDE, 2 * Z, LANES)
-
-    pl.semaphore_wait(barrier, WIDE - 1 + SEGMENTS * Z - 1 + Y * (LAG_PARTS - 1))
-
-    for kind in range(1 + PARTS):
+    panel_out[...] = select_rows(panel_place == panel_at, records).reshape(WIDE * NEAR, 8, LANES)
+    outgoing[...] = select_rows(place == series_at, records).reshape(PARTS, WIDE, 2 * Z, LANES)
+
+    pl.semaphore_wait(barrier, WIDE * NEAR - 1 + Z - NEAR + Y * (LAG_PARTS - 1) + Z * segment)
+
+    kept = pl.ds(0, PARTS * KEPT)
+    for step in range(1, WIDE * NEAR):
+        at, peer = near_peer(step)
+        copy(panel_out.at[at, kept], panel_in.at[near, kept], 0, chan=peer).start()
+    panel_in[near] = panel_out[near]
+
+    @pl.when(segment == 1)
+    def _():
+        for step in range(Z):
+            pl.semaphore_signal(
+                late_sem,
+                inc=1,
+                device_id={"chan": owner(y, step, core), "seg": 0},
+                device_id_type=MESH,
+            )
+
+    for part in range(PARTS):
         for step in range(1, WIDE):
             at = (wide + step) % WIDE
             copy(
-                outgoing.at[kind, at], across_plane.at[kind, wide], kind, chan=plane_peer(step)
+                outgoing.at[part, at],
+                across_plane.at[part, wide],
+                1 + part,
+                chan=plane_peer(step),
             ).start()
-        across_plane[kind, wide] = outgoing[kind, wide]
+        across_plane[part, wide] = outgoing[part, wide]
 
     lists = lists_ref[...].astype(jnp.float32)
     lists = jnp.transpose(jnp.concatenate([lists, lists], axis=0)).astype(jnp.int32)
@@ -191,22 +221,35 @@
     )
     by_line = right == (down // 2 % WIDE * Z + down // (2 * WIDE)) * 2 + down % 2
 
-    seven_plane = [across_plane.at[kind, pl.ds(0, WIDE - 1)] for kind in range(1 + PARTS)]
+    seven_plane = [across_plane.at[part, pl.ds(0, WIDE - 1)] for part in range(PARTS)]
+    near_others = panel_in.at[pl.ds(0, WIDE * NEAR - 1), kept]
     seven_line = along_line.at[0, pl.ds(0, Z - 1)]
 
-    wait_all(seven_plane[0], 0)
-    sums = jnp.sum(across_plane[0], axis=0)
-    for at in range(Z):
-        sums_out[at] = sums[2 * at : 2 * at + 2]
+    wait_all(near_others, 0)
+    sums[along, kept] = jnp.sum(panel_in[:, kept], axis=0)
     for step in range(1, Z):
-        at = (z + step) % Z
-        copy(sums_out.at[at], sums_in.at[z], 3, chan=owner(y, at, core)).start()
-    sums_in[z] = sums_out[z]
+        copy(
+            sums.at[along, kept], sums.at[along, kept], 3, chan=owner(y, (z + step) % Z, core)
+        ).start()
+
+    def send_sums_over():
+        for step in range(Z):
+            copy(
+                sums.at[along, kept],
+                sums.at[along, kept],
+                15,
+                chan=owner(y, (z + step) % Z, core),
+                seg=1 - segment,
+            ).start()
+
+    @pl.when(segment == 1)
+    def _():
+        send_sums_over()
 
     def send_line(part):
-        wait_all(seven_plane[1 + part], 1 + part)
+        wait_all(seven_plane[part], 1 + part)
         line_out[part] = select_rows(
-            by_line, across_plane[1 + part].reshape(ROWS, LANES)
+            by_line, across_plane[part].reshape(ROWS, LANES)
         ).reshape(Z, 2 * WIDE, LANES)
         for step in range(1, Z):
             at = (z + step) % Z
@@ -218,12 +261,6 @@
     send_line(0)
     send_line(1)
 
-    seven_sums = sums_in.at[pl.ds(0, Z - 1)]
-    wait_all(seven_sums, 3)
-    rows_z[along] = jnp.sum(sums_in[...], axis=0)
-    for step in range(1, SEGMENTS * Z):
-        copy(rows_z.at[along], rows_z.at[along], 6, **line_peer(step)).start()
-
     own_tile = (segment * LAG_PARTS + lag) * PARTS
     other_tile = ((1 - segment) * LAG_PARTS + lag) * PARTS
     swaps = [
@@ -241,49 +278,62 @@
         wait_all(seven_line, 4 + part)
         placed = select_rows(placing, along_line[part].reshape(ROWS, LANES))
         theirs[part] = placed[HALF:]
-
-        @pl.when(segment == 1)
-        def _():
-            swaps[part].start()
-
+        if part == 0:
+
+            @pl.when(segment == 0)
+            def _():
+                pl.semaphore_wait(late_sem, Z)
+
+        swaps[part].start()
         series_ref[own_tile + part] = placed[:HALF]
         forward(own_tile + part, 11 + part)
 
     place_part(0)
-
-    z_rows = rows_z.at[pl.ds(0, SEGMENTS * Z - 1)]
-    wait_all(z_rows, 6)
+    place_part(1)
+
+    @pl.when(segment == 0)
+    def _():
+        send_sums_over()
+
     lag_tiles = pl.ds(lag * PARTS, PARTS)
     group_rows = pl.ds(pl.multiple_of((core * Y + y) * Z, Z), Z)
-    for at in range(SEGMENTS):
-        for part in range(PARTS):
-            panel_ref[at, lag * PARTS + part, group_rows, :] = rows_z[
-                at * Z : (at + 1) * Z, part, :
-            ]
-    group_tiles = panel_ref.at[:, lag_tiles, group_rows]
-    for y_step in range(Y):
-        for step in range(LAG_PARTS):
-            if y_step or step:
-                copy(
-                    group_tiles,
-                    group_tiles,
-                    7,
-                    chan=owner((y + y_step) % Y, z, core),
-                    lag=(lag + step) % LAG_PARTS,
-                ).start()
-
-    place_part(1)
+
+    def send_group(at, number):
+        for low in range(NEAR):
+            total = sums[at * Z + low, kept]
+            for high in range(1, Z // NEAR):
+                total = total + sums[at * Z + high * NEAR + low, kept]
+            rows = pl.ds((core * Y + y) * Z + low * KEPT, KEPT)
+            for part in range(PARTS):
+                panel_ref[at, lag * PARTS + part, rows, :] = total[
+                    part * KEPT : (part + 1) * KEPT
+                ]
+        group_tiles = panel_ref.at[at, lag_tiles, group_rows]
+        for y_step in range(Y):
+            for step in range(LAG_PARTS):
+                if y_step or step:
+                    copy(
+                        group_tiles,
+                        group_tiles,
+                        number,
+                        chan=owner((y + y_step) % Y, z, core),
+                        lag=(lag + step) % LAG_PARTS,
+                    ).start()
+
+    seven_sums = sums.at[pl.ds(0, Z - 1), kept]
+    eight_sums = sums.at[pl.ds(0, Z), kept]
+    wait_all(seven_sums, 3)
+    send_group(segment, 7)
+    wait_all(eight_sums, 15)
+    send_group(1 - segment, 16)
+
     for part in range(PARTS):
         swaps[part].wait_recv()
         forward(other_tile + part, 13 + part)
 
-    @pl.when(segment == 0)
-    def _():
-        for part in range(PARTS):
-            swaps[part].start()
-
-    xy_tiles = panel_ref.at[:, pl.ds(0, 5), pl.ds(0, 6 * Z)]
+    xy_tiles = panel_ref.at[0, pl.ds(0, 5), pl.ds(0, 6 * Z)]
     wait_all(xy_tiles, 7)
+    wait_all(xy_tiles, 16)
     core_rows = pl.ds(pl.multiple_of(core * Y * Z, Y * Z), Y * Z)
     half_panel = panel_ref.at[:, :, core_rows]
     across = copy(half_panel, half_panel, 8, chan=owner(y, z, 1 - core))
@@ -292,16 +342,19 @@
     for number in range(11, 15):
         wait_all(three, number)
     across.wait()
-    for kind in range(1 + PARTS):
-        wait_sent(seven_plane[kind], kind)
+    wait_sent(near_others, 0)
     wait_sent(seven_sums, 3)
+    wait_sent(eight_sums, 15)
     for part in range(PARTS):
+        wait_sent(seven_plane[part], 1 + part)
         wait_sent(seven_line, 4 + part)
-        swaps[part].wait_send()
-    wait_sent(z_rows, 6)
     wait_sent(xy_tiles, 7)
+    wait_sent(xy_tiles, 16)
     for number in range(11, 15):
         wait_sent(three, number)
+
+    for part in range(PARTS):
+        swaps[part].wait_send()
 
 
 def correlate(series_ref, panel_ref, out_ref, windows_high, windows_low, shifts_high, shifts_low):
@@ -354,17 +407,18 @@
             pltpu.VMEM((ROWS * PARTS, LANES), jnp.float32),
             pltpu.VMEM((OWNERS, ROWS), jnp.int32),
             pltpu.VMEM((1, REF), jnp.int32),
-            pltpu.VMEM((1 + PARTS, WIDE, 2 * Z, LANES), jnp.float32),
-            pltpu.VMEM((1 + PARTS, WIDE, 2 * Z, LANES), jnp.float32),
+            pltpu.VMEM((WIDE * NEAR, 8, LANES), jnp.float32),
+            pltpu.VMEM((WIDE * NEAR, 8, LANES), jnp.float32),
+            pltpu.VMEM((PARTS, WIDE, 2 * Z, LANES), jnp.float32),
+            pltpu.VMEM((PARTS, WIDE, 2 * Z, LANES), jnp.float32),
             pltpu.VMEM((PARTS, Z, 2 * WIDE, LANES), jnp.float32),
             pltpu.VMEM((PARTS, Z, 2 * WIDE, LANES), jnp.float32),
-            pltpu.VMEM((Z, PARTS, LANES), jnp.float32),
-            pltpu.VMEM((Z, PARTS, LANES), jnp.float32),
-            pltpu.VMEM((SEGMENTS * Z, PARTS, LANES), jnp.float32),
+            pltpu.VMEM((SEGMENTS * Z, 8, LANES), jnp.float32),
             pltpu.VMEM((PARTS, HALF, LANES), jnp.float32),
+            pltpu.SemaphoreType.REGULAR,
             pltpu.SemaphoreType.DMA((3,)),
-            pltpu.SemaphoreType.DMA((15,)),
-            pltpu.SemaphoreType.DMA((15,)),
+            pltpu.SemaphoreType.DMA((17,)),
+            pltpu.SemaphoreType.DMA((17,)),
         ],
         compiler_params=pltpu.CompilerParams(
             collective_id=0, has_side_effects=True, vmem_limit_bytes=32 * 1024 * 1024

time: 53.3 us -> 47.5 us (0.89)
  the two profiles are of different devices: /device:TPU:448 before, /device:TPU:2 now
where the time goes in v5:
time: 47.5 us; the launch traced here: 47.3 us
  Pallas kernels  47.3 us (100%)
    pallas_call x1, Pallas kernels, shards(): pl.pallas_call(exchange, out_shape=[jax.ShapeDtypeStruct((TILES, HALF, LA...  43.7 us
    pallas_call x1, Pallas kernels, shards(): pl.pallas_call(correlate, out_shape=jax.ShapeDtypeStruct((HALF, lag_width...  3.65 us

profile of v5, /device:TPU:2, one launch (start us, length us, event | category | flops | bytes accessed | tf_op | source)
XLA Modules:
  0.0 47.3 jit_solution(14642399508401073258)
XLA Ops:
  0.0 43.7 %exchange.1 = (f32[16,64,128]{2,1,0:T(8,128)S(1)}, f32[2,8,64,128]{3,2,1,0:T(8,128)S(1)}) custom-call(f32[256,128]{1,0:T(8,128)} %bitcast.3, s32[64,128]{1,0:T(8,128)} %bitcast.4, s32[1,64]{1,0:T(1,128)} %bitcast.5), custom_call_target="tpu_custom_call" | custom-call | tf_op jit(solution)/shard_map/exchange/pallas_call | solution.py:398
  43.7 3.6 %correlate.1 = f32[64,2048]{1,0:T(8,128)} custom-call(f32[16,64,128]{2,1,0:T(8,128)S(1)} %get-tuple-element.7.series_ref, f32[2,8,64,128]{3,2,1,0:T(8,128)S(1)} %get-tuple-element.8.panel_ref), custom_call_target="tpu_custom_call" | custom-call | tf_op jit(solution)/shard_map/correlate/pallas_call | solution.py:439

commit v6 on v5

--- a/solution.py
+++ b/solution.py
@@ -22,7 +22,7 @@
 LAG_PARTS = 4
 Y, Z, CORES = 4, 8, 2
 WIDE = Y * CORES
-NEAR = 2
+NEAR = 4
 KEPT = Z // NEAR
 PARTS = 2
 
@@ -132,14 +132,14 @@
         for step in range(Z):
             greet(chan=owner(y, step, core), seg=1)
 
-    for step in range(1, WIDE * NEAR):
-        greet(chan=near_peer(step)[1])
     for step in range(1, Z // NEAR):
         for at in range(NEAR):
             greet(chan=owner(y, (first_near + step * NEAR + at) % Z, core))
     for y_step in range(Y):
         for step in range(1, LAG_PARTS):
             greet(chan=owner((y + y_step) % Y, z, core), lag=(lag + step) % LAG_PARTS)
+    for step in range(1, WIDE * NEAR):
+        greet(chan=near_peer(step)[1])
     for load in loads:
         load.wait()
 
@@ -173,22 +173,6 @@
 
     pl.semaphore_wait(barrier, WIDE * NEAR - 1 + Z - NEAR + Y * (LAG_PARTS - 1) + Z * segment)
 
-    kept = pl.ds(0, PARTS * KEPT)
-    for step in range(1, WIDE * NEAR):
-        at, peer = near_peer(step)
-        copy(panel_out.at[at, kept], panel_in.at[near, kept], 0, chan=peer).start()
-    panel_in[near] = panel_out[near]
-
-    @pl.when(segment == 1)
-    def _():
-        for step in range(Z):
-            pl.semaphore_signal(
-                late_sem,
-                inc=1,
-                device_id={"chan": owner(y, step, core), "seg": 0},
-                device_id_type=MESH,
-            )
-
     for part in range(PARTS):
         for step in range(1, WIDE):
             at = (wide + step) % WIDE
@@ -199,6 +183,22 @@
                 chan=plane_peer(step),
             ).start()
         across_plane[part, wide] = outgoing[part, wide]
+
+    kept = pl.ds(0, PARTS * KEPT)
+    for step in range(1, WIDE * NEAR):
+        at, peer = near_peer(step)
+        copy(panel_out.at[at, kept], panel_in.at[near, kept], 0, chan=peer).start()
+    panel_in[near] = panel_out[near]
+
+    @pl.when(segment == 1)
+    def _():
+        for step in range(Z):
+            pl.semaphore_signal(
+                late_sem,
+                inc=1,
+                device_id={"chan": owner(y, step, core), "seg": 0},
+                device_id_type=MESH,
+            )
 
     lists = lists_ref[...].astype(jnp.float32)
     lists = jnp.transpose(jnp.concatenate([lists, lists], axis=0)).astype(jnp.int32)
@@ -225,27 +225,6 @@
     near_others = panel_in.at[pl.ds(0, WIDE * NEAR - 1), kept]
     seven_line = along_line.at[0, pl.ds(0, Z - 1)]
 
-    wait_all(near_others, 0)
-    sums[along, kept] = jnp.sum(panel_in[:, kept], axis=0)
-    for step in range(1, Z):
-        copy(
-            sums.at[along, kept], sums.at[along, kept], 3, chan=owner(y, (z + step) % Z, core)
-        ).start()
-
-    def send_sums_over():
-        for step in range(Z):
-            copy(
-                sums.at[along, kept],
-                sums.at[along, kept],
-                15,
-                chan=owner(y, (z + step) % Z, core),
-                seg=1 - segment,
-            ).start()
-
-    @pl.when(segment == 1)
-    def _():
-        send_sums_over()
-
     def send_line(part):
         wait_all(seven_plane[part], 1 + part)
         line_out[part] = select_rows(
@@ -259,6 +238,27 @@
         along_line[part, z] = line_out[part, z]
 
     send_line(0)
+    wait_all(near_others, 0)
+    sums[along, kept] = jnp.sum(panel_in[:, kept], axis=0)
+    for step in range(1, Z):
+        copy(
+            sums.at[along, kept], sums.at[along, kept], 3, chan=owner(y, (z + step) % Z, core)
+        ).start()
+
+    def send_sums_over():
+        for step in range(Z):
+            copy(
+                sums.at[along, kept],
+                sums.at[along, kept],
+                15,
+                chan=owner(y, (z + step) % Z, core),
+                seg=1 - segment,
+            ).start()
+
+    @pl.when(segment == 1)
+    def _():
+        send_sums_over()
+
     send_line(1)
 
     own_tile = (segment * LAG_PARTS + lag) * PARTS
@@ -284,7 +284,13 @@
             def _():
                 pl.semaphore_wait(late_sem, Z)
 
-        swaps[part].start()
+            swaps[part].start()
+        else:
+
+            @pl.when(segment == 1)
+            def _():
+                swaps[part].start()
+
         series_ref[own_tile + part] = placed[:HALF]
         forward(own_tile + part, 11 + part)
 
@@ -330,6 +336,12 @@
     for part in range(PARTS):
         swaps[part].wait_recv()
         forward(other_tile + part, 13 + part)
+        if part == 0:
+
+            @pl.when(segment == 0)
+            def _():
+                swaps[1].start()
+
 
     xy_tiles = panel_ref.at[0, pl.ds(0, 5), pl.ds(0, 6 * Z)]
     wait_all(xy_tiles, 7)

time: 47.5 us -> 44.6 us (0.939)
  the two profiles are of different devices: /device:TPU:2 before, /device:TPU:1 now
where the time goes in v6:
time: 44.6 us; the launch traced here: 44.3 us
  Pallas kernels  44.3 us (99%)
    pallas_call x1, Pallas kernels, shards(): pl.pallas_call(exchange, out_shape=[jax.ShapeDtypeStruct((TILES, HALF, LA...  40.7 us
    pallas_call x1, Pallas kernels, shards(): pl.pallas_call(correlate, out_shape=jax.ShapeDtypeStruct((HALF, lag_width...  3.65 us

profile of v6, /device:TPU:1, one launch (start us, length us, event | category | flops | bytes accessed | tf_op | source)
XLA Modules:
  0.0 44.3 jit_solution(5649602666387164169)
XLA Ops:
  0.0 40.7 %exchange.1 = (f32[16,64,128]{2,1,0:T(8,128)S(1)}, f32[2,8,64,128]{3,2,1,0:T(8,128)S(1)}) custom-call(f32[256,128]{1,0:T(8,128)} %bitcast.3, s32[64,128]{1,0:T(8,128)} %bitcast.4, s32[1,64]{1,0:T(1,128)} %bitcast.5), custom_call_target="tpu_custom_call" | custom-call | tf_op jit(solution)/shard_map/exchange/pallas_call | solution.py:410
  40.7 3.6 %correlate.1 = f32[64,2048]{1,0:T(8,128)} custom-call(f32[16,64,128]{2,1,0:T(8,128)S(1)} %get-tuple-element.7.series_ref, f32[2,8,64,128]{3,2,1,0:T(8,128)S(1)} %get-tuple-element.8.panel_ref), custom_call_target="tpu_custom_call" | custom-call | tf_op jit(solution)/shard_map/correlate/pallas_call | solution.py:451

commit v7 on v5

--- a/solution.py
+++ b/solution.py
@@ -22,7 +22,9 @@
 LAG_PARTS = 4
 Y, Z, CORES = 4, 8, 2
 WIDE = Y * CORES
-NEAR = 2
+NEAR = 4
+PIECES = 2
+HELD = 1
 KEPT = Z // NEAR
 PARTS = 2
 
@@ -62,9 +64,7 @@
     panel_out,
     panel_in,
     outgoing,
-    across_plane,
-    line_out,
-    along_line,
+    arrived,
     sums,
     theirs,
     late_sem,
@@ -85,10 +85,6 @@
 
     wide = y * CORES + core
 
-    def plane_peer(step):
-        at = (wide + step) % WIDE
-        return owner(at // CORES, z, at % CORES)
-
     first_near = z // NEAR * NEAR
     near = wide * NEAR + z % NEAR
 
@@ -132,11 +128,11 @@
         for step in range(Z):
             greet(chan=owner(y, step, core), seg=1)
 
-    for step in range(1, WIDE * NEAR):
-        greet(chan=near_peer(step)[1])
-    for step in range(1, Z // NEAR):
-        for at in range(NEAR):
-            greet(chan=owner(y, (first_near + step * NEAR + at) % Z, core))
+    def greet_owner(step, carry):
+        greet(chan=(me + step) % OWNERS)
+        return carry
+
+    lax.fori_loop(1, OWNERS, greet_owner, 0)
     for y_step in range(Y):
         for step in range(1, LAG_PARTS):
             greet(chan=owner((y + y_step) % Y, z, core), lag=(lag + step) % LAG_PARTS)
@@ -159,25 +155,37 @@
         jnp.where(refs_down == own, target * 8 + number % KEPT + 1, 0), axis=0, keepdims=True
     )
     panel_at = panel_at - 1
-    own_wide = own_block // (Z * CORES) * CORES + own_block % CORES
-    series_at = (own_wide * Z + own_block // CORES % Z) * 2 + rank
-    series_at = jnp.concatenate([series_at, series_at + ROWS], axis=1)
+    series_at = own_block * 8 + rank
+    series_at = jnp.concatenate([series_at, series_at + 2], axis=1)
     panel_at = jnp.concatenate([panel_at, jnp.where(panel_at < 0, -1, panel_at + KEPT)], axis=1)
-    place = iota((PARTS * ROWS, PARTS * ROWS), 0)
+    place = iota((OWNERS * 8, PARTS * ROWS), 0)
     panel_place = iota((WIDE * NEAR * 8, PARTS * ROWS), 0)
     records = jnp.concatenate(
         [records_ref[pl.ds(part, ROWS, PARTS), :] for part in range(PARTS)], axis=0
     )
     panel_out[...] = select_rows(panel_place == panel_at, records).reshape(WIDE * NEAR, 8, LANES)
-    outgoing[...] = select_rows(place == series_at, records).reshape(PARTS, WIDE, 2 * Z, LANES)
-
-    pl.semaphore_wait(barrier, WIDE * NEAR - 1 + Z - NEAR + Y * (LAG_PARTS - 1) + Z * segment)
-
+    outgoing[...] = select_rows(place == series_at, records).reshape(OWNERS, 8, LANES)
+
+    pl.semaphore_wait(barrier, OWNERS - 1 + Y * (LAG_PARTS - 1) + Z * segment)
+
+    def send_part(part):
+        pair = pl.ds(2 * part, 2)
+
+        def send_owner(step, carry):
+            peer = (me + step) % OWNERS
+            copy(outgoing.at[peer, pair], arrived.at[me, pair], 1 + part, chan=peer).start()
+            return carry
+
+        lax.fori_loop(1, OWNERS, send_owner, 0)
+
+    send_part(0)
     kept = pl.ds(0, PARTS * KEPT)
     for step in range(1, WIDE * NEAR):
         at, peer = near_peer(step)
         copy(panel_out.at[at, kept], panel_in.at[near, kept], 0, chan=peer).start()
     panel_in[near] = panel_out[near]
+    send_part(1)
+    arrived[me] = outgoing[me]
 
     @pl.when(segment == 1)
     def _():
@@ -189,17 +197,6 @@
                 device_id_type=MESH,
             )
 
-    for part in range(PARTS):
-        for step in range(1, WIDE):
-            at = (wide + step) % WIDE
-            copy(
-                outgoing.at[part, at],
-                across_plane.at[part, wide],
-                1 + part,
-                chan=plane_peer(step),
-            ).start()
-        across_plane[part, wide] = outgoing[part, wide]
-
     lists = lists_ref[...].astype(jnp.float32)
     lists = jnp.transpose(jnp.concatenate([lists, lists], axis=0)).astype(jnp.int32)
     inside = lists // ROWS == me
@@ -207,23 +204,9 @@
     second = jnp.max(jnp.where(inside, lists, -1), axis=0, keepdims=True)
     ids = jnp.where(iota((1, ROWS), 1) < OWNERS, first, second)
     turned = me * ROWS + (iota((ROWS, ROWS), 0) + segment * HALF) % ROWS
-    down, right = iota((ROWS, ROWS), 0), iota((ROWS, ROWS), 1)
-    right_wide = right // 2 % WIDE
-    right_owner = owner(right_wide // CORES, right // (2 * WIDE), right_wide % CORES)
-    reorder = jnp.where(down == right % 2 * OWNERS + right_owner, 1.0, 0.0).astype(jnp.bfloat16)
-    placing = (
-        jnp.dot(
-            jnp.where(turned == ids, 1.0, 0.0).astype(jnp.bfloat16),
-            reorder,
-            preferred_element_type=jnp.float32,
-        )
-        > 0.5
-    )
-    by_line = right == (down // 2 % WIDE * Z + down // (2 * WIDE)) * 2 + down % 2
-
-    seven_plane = [across_plane.at[part, pl.ds(0, WIDE - 1)] for part in range(PARTS)]
+    placing = turned == ids
+    others = [arrived.at[pl.ds(0, OWNERS - 1), pl.ds(2 * part, 2)] for part in range(PARTS)]
     near_others = panel_in.at[pl.ds(0, WIDE * NEAR - 1), kept]
-    seven_line = along_line.at[0, pl.ds(0, Z - 1)]
 
     wait_all(near_others, 0)
     sums[along, kept] = jnp.sum(panel_in[:, kept], axis=0)
@@ -246,45 +229,47 @@
     def _():
         send_sums_over()
 
-    def send_line(part):
-        wait_all(seven_plane[part], 1 + part)
-        line_out[part] = select_rows(
-            by_line, across_plane[part].reshape(ROWS, LANES)
-        ).reshape(Z, 2 * WIDE, LANES)
-        for step in range(1, Z):
-            at = (z + step) % Z
-            copy(
-                line_out.at[part, at], along_line.at[part, z], 4 + part, chan=owner(y, at, core)
-            ).start()
-        along_line[part, z] = line_out[part, z]
-
-    send_line(0)
-    send_line(1)
 
     own_tile = (segment * LAG_PARTS + lag) * PARTS
     other_tile = ((1 - segment) * LAG_PARTS + lag) * PARTS
+    pieces = [
+        (part, pl.ds(piece * HALF // PIECES, HALF // PIECES))
+        for part in range(PARTS)
+        for piece in range(PIECES)
+    ]
     swaps = [
-        copy(theirs.at[part], series_ref.at[own_tile + part], 9 + part, seg=1 - segment)
-        for part in range(PARTS)
+        copy(theirs.at[part, rows], series_ref.at[own_tile + part, rows], 17 + at, seg=1 - segment)
+        for at, (part, rows) in enumerate(pieces)
     ]
 
-    def forward(tile, number):
+    def forward(tile, number, rows=pl.ds(0, HALF)):
+        block = series_ref.at[tile, rows]
         for step in range(1, LAG_PARTS):
-            copy(
-                series_ref.at[tile], series_ref.at[tile], number, lag=(lag + step) % LAG_PARTS
-            ).start()
+            copy(block, block, number, lag=(lag + step) % LAG_PARTS).start()
 
     def place_part(part):
-        wait_all(seven_line, 4 + part)
-        placed = select_rows(placing, along_line[part].reshape(ROWS, LANES))
+        wait_all(others[part], 1 + part)
+        placed = select_rows(
+            placing,
+            jnp.concatenate([arrived[:, 2 * part + slot, :] for slot in range(2)], axis=0),
+        )
         theirs[part] = placed[HALF:]
+
+        def start_swaps():
+            for at, (piece_part, _) in enumerate(pieces):
+                if piece_part == part:
+                    swaps[at].start()
+
         if part == 0:
 
             @pl.when(segment == 0)
             def _():
                 pl.semaphore_wait(late_sem, Z)
 
-        swaps[part].start()
+            start_swaps()
+        else:
+            pl.when(segment == 1)(start_swaps)
+
         series_ref[own_tile + part] = placed[:HALF]
         forward(own_tile + part, 11 + part)
 
@@ -327,9 +312,15 @@
     wait_all(eight_sums, 15)
     send_group(1 - segment, 16)
 
-    for part in range(PARTS):
-        swaps[part].wait_recv()
-        forward(other_tile + part, 13 + part)
+    for at, (part, rows) in enumerate(pieces):
+        swaps[at].wait_recv()
+        forward(other_tile + part, 17 + len(pieces) + at, rows)
+        if at == HELD:
+
+            @pl.when(segment == 0)
+            def _():
+                for swap in swaps[PIECES:]:
+                    swap.start()
 
     xy_tiles = panel_ref.at[0, pl.ds(0, 5), pl.ds(0, 6 * Z)]
     wait_all(xy_tiles, 7)
@@ -339,22 +330,25 @@
     across = copy(half_panel, half_panel, 8, chan=owner(y, z, 1 - core))
     across.start()
     three = series_ref.at[pl.ds(0, LAG_PARTS - 1)]
-    for number in range(11, 15):
+    for number in (11, 12):
         wait_all(three, number)
+    three_pieces = series_ref.at[pl.ds(0, LAG_PARTS - 1), pl.ds(0, HALF // PIECES)]
+    for at in range(len(pieces)):
+        wait_all(three_pieces, 17 + len(pieces) + at)
     across.wait()
     wait_sent(near_others, 0)
     wait_sent(seven_sums, 3)
     wait_sent(eight_sums, 15)
     for part in range(PARTS):
-        wait_sent(seven_plane[part], 1 + part)
-        wait_sent(seven_line, 4 + part)
+        wait_sent(others[part], 1 + part)
     wait_sent(xy_tiles, 7)
     wait_sent(xy_tiles, 16)
-    for number in range(11, 15):
+    for number in (11, 12):
         wait_sent(three, number)
-
-    for part in range(PARTS):
-        swaps[part].wait_send()
+    for at in range(len(pieces)):
+        wait_sent(three_pieces, 17 + len(pieces) + at)
+    for swap in swaps:
+        swap.wait_send()
 
 
 def correlate(series_ref, panel_ref, out_ref, windows_high, windows_low, shifts_high, shifts_low):
@@ -409,16 +403,14 @@
             pltpu.VMEM((1, REF), jnp.int32),
             pltpu.VMEM((WIDE * NEAR, 8, LANES), jnp.float32),
             pltpu.VMEM((WIDE * NEAR, 8, LANES), jnp.float32),
-            pltpu.VMEM((PARTS, WIDE, 2 * Z, LANES), jnp.float32),
-            pltpu.VMEM((PARTS, WIDE, 2 * Z, LANES), jnp.float32),
-            pltpu.VMEM((PARTS, Z, 2 * WIDE, LANES), jnp.float32),
-            pltpu.VMEM((PARTS, Z, 2 * WIDE, LANES), jnp.float32),
+            pltpu.VMEM((OWNERS, 8, LANES), jnp.float32),
+            pltpu.VMEM((OWNERS, 8, LANES), jnp.float32),
             pltpu.VMEM((SEGMENTS * Z, 8, LANES), jnp.float32),
             pltpu.VMEM((PARTS, HALF, LANES), jnp.float32),
             pltpu.SemaphoreType.REGULAR,
             pltpu.SemaphoreType.DMA((3,)),
-            pltpu.SemaphoreType.DMA((17,)),
-            pltpu.SemaphoreType.DMA((17,)),
+            pltpu.SemaphoreType.DMA((25,)),
+            pltpu.SemaphoreType.DMA((25,)),
         ],
         compiler_params=pltpu.CompilerParams(
             collective_id=0, has_side_effects=True, vmem_limit_bytes=32 * 1024 * 1024

time: 47.5 us -> 44.1 us (0.928)
  the two profiles are of different devices: /device:TPU:2 before, /device:TPU:1 now
where the time goes in v7:
time: 44.1 us; the launch traced here: 44 us
  Pallas kernels  44 us (100%)
    pallas_call x1, Pallas kernels, shards(): pl.pallas_call(exchange, out_shape=[jax.ShapeDtypeStruct((TILES, HALF, LA...  40.3 us
    pallas_call x1, Pallas kernels, shards(): pl.pallas_call(correlate, out_shape=jax.ShapeDtypeStruct((HALF, lag_width...  3.65 us

profile of v7, /device:TPU:1, one launch (start us, length us, event | category | flops | bytes accessed | tf_op | source)
XLA Modules:
  0.0 44.0 jit_solution(11844243243403643416)
XLA Ops:
  0.0 40.3 %exchange.1 = (f32[16,64,128]{2,1,0:T(8,128)S(1)}, f32[2,8,64,128]{3,2,1,0:T(8,128)S(1)}) custom-call(f32[256,128]{1,0:T(8,128)} %bitcast.3, s32[64,128]{1,0:T(8,128)} %bitcast.4, s32[1,64]{1,0:T(1,128)} %bitcast.5), custom_call_target="tpu_custom_call" | custom-call | tf_op jit(solution)/shard_map/exchange/pallas_call | solution.py:392
  40.3 3.6 %correlate.1 = f32[64,2048]{1,0:T(8,128)} custom-call(f32[16,64,128]{2,1,0:T(8,128)S(1)} %get-tuple-element.7.series_ref, f32[2,8,64,128]{3,2,1,0:T(8,128)S(1)} %get-tuple-element.8.panel_ref), custom_call_target="tpu_custom_call" | custom-call | tf_op jit(solution)/shard_map/correlate/pallas_call | solution.py:431

commit v8 on v7

--- a/solution.py
+++ b/solution.py
@@ -351,7 +351,7 @@
         swap.wait_send()
 
 
-def correlate(series_ref, panel_ref, out_ref, windows_high, windows_low, shifts_high, shifts_low):
+def correlate(series_ref, panel_ref, out_ref, windows, shifts_high, shifts_low):
     lag_width = LAGS // LAG_PARTS
     rows = series_ref.shape[1]
     groups = lag_width // COLUMN_LAGS
@@ -371,12 +371,13 @@
     for group in range(groups):
         lag = group * COLUMN_LAGS
         high, low = split(pltpu.roll(series, SAMPLES - lag, 1) if lag else series)
-        windows_high[pl.ds(group * rows, rows), :] = high
-        windows_low[pl.ds(group * rows, rows), :] = low
+        windows[pl.ds(group * rows, rows), :] = high
+        windows[pl.ds((groups + group) * rows, rows), :] = low
+    both = transposed_dot(windows[...], shifts_high[...])
     total = (
-        transposed_dot(windows_high[...], shifts_high[...])
-        + transposed_dot(windows_high[...], shifts_low[...])
-        + transposed_dot(windows_low[...], shifts_high[...])
+        both[: groups * rows]
+        + transposed_dot(windows[pl.ds(0, groups * rows), :], shifts_low[...])
+        + both[groups * rows :]
     )
     width = COLUMN_LAGS * REF
     for group in range(groups):
@@ -433,7 +434,7 @@
         out_shape=jax.ShapeDtypeStruct((HALF, lag_width * REF), jnp.float32),
         in_specs=[VMEM] * 2,
         out_specs=VMEM,
-        scratch_shapes=[pltpu.VMEM((groups * HALF, SAMPLES), jnp.bfloat16)] * 2
+        scratch_shapes=[pltpu.VMEM((2 * groups * HALF, SAMPLES), jnp.bfloat16)]
         + [pltpu.VMEM((COLUMN_LAGS * REF, SAMPLES), jnp.bfloat16)] * 2,
         compiler_params=pltpu.CompilerParams(vmem_limit_bytes=32 * 1024 * 1024),
         name="correlate",

time: 44.1 us -> 43.6 us (0.989)
  Pallas kernels: 44 us -> 43.5 us
    pallas_call x1, Pallas kernels: 3.65 us -> 3.17 us  [shards(): pl.pallas_call(correlate, out_shape=jax.ShapeDtypeStruct((HALF, lag_width...]
where the time goes in v8:
time: 43.6 us; the launch traced here: 43.5 us
  Pallas kernels  43.5 us (100%)
    pallas_call x1, Pallas kernels, shards(): pl.pallas_call(exchange, out_shape=[jax.ShapeDtypeStruct((TILES, HALF, LA...  40.3 us
    pallas_call x1, Pallas kernels, shards(): pl.pallas_call(correlate, out_shape=jax.ShapeDtypeStruct((HALF, lag_width...  3.17 us

profile of v8, /device:TPU:1, one launch (start us, length us, event | category | flops | bytes accessed | tf_op | source)
XLA Modules:
  0.0 43.5 jit_solution(5555178198386734517)
XLA Ops:
  0.0 40.3 %exchange.1 = (f32[16,64,128]{2,1,0:T(8,128)S(1)}, f32[2,8,64,128]{3,2,1,0:T(8,128)S(1)}) custom-call(f32[256,128]{1,0:T(8,128)} %bitcast.3, s32[64,128]{1,0:T(8,128)} %bitcast.4, s32[1,64]{1,0:T(1,128)} %bitcast.5), custom_call_target="tpu_custom_call" | custom-call | tf_op jit(solution)/shard_map/exchange/pallas_call | solution.py:393
  40.3 3.2 %correlate.1 = f32[64,2048]{1,0:T(8,128)} custom-call(f32[16,64,128]{2,1,0:T(8,128)S(1)} %get-tuple-element.7.series_ref, f32[2,8,64,128]{3,2,1,0:T(8,128)S(1)} %get-tuple-element.8.panel_ref), custom_call_target="tpu_custom_call" | custom-call | tf_op jit(solution)/shard_map/correlate/pallas_call | solution.py:432
